TPU v7x, 32 devices: a whole 2x2x4 slice. The times are simulated.
32 devices in a mesh: seq: 2 (over x), fsdp: 16 (over z, y, core).
Axes of the slice: x: 2, y: 2, z: 4, core: 2. Of those that a mesh axis runs over, the one named last changes fastest.
Arguments:
- layer_input: bfloat16 [16, 1024, 768], P('fsdp', 'seq'), may hold values from -6 to 6
- segment_ids: int32 [16, 1024], P('fsdp'), may hold values from 0 to 5, never falling along the last dimension, each value on 1 to 256 neighbouring positions
- key_valid: int32 [16, 1024], P('fsdp'), may hold values 0 or 1
- first_gain: bfloat16 [2, 768], P(None, 'fsdp'), may hold values from 0.25 to 1.75
- first_shift: bfloat16 [2, 768], P(None, 'fsdp'), may hold values from -1.75 to 1.75
- input_weight: bfloat16 [2, 768, 2304], P(None, 'fsdp'), may hold values from -0.21875 to 0.21875
- query_bias: bfloat16 [2, 768], P(None, 'fsdp'), may hold values from -3 to 3
- value_bias: bfloat16 [2, 768], P(None, 'fsdp'), may hold values from -3 to 3
- output_weight: bfloat16 [2, 768, 768], P(None, 'fsdp'), may hold values from -1.25 to 1.25
- output_bias: bfloat16 [2, 768], P(None, 'fsdp'), may hold values from -1.75 to 1.75
- second_gain: bfloat16 [2, 768], P(None, 'fsdp'), may hold values from 0.25 to 1.75
- second_shift: bfloat16 [2, 768], P(None, 'fsdp'), may hold values from -1.75 to 1.75
- up_weight: bfloat16 [2, 768, 3072], P(None, 'fsdp'), may hold values from -0.21875 to 0.21875
- up_bias: bfloat16 [2, 3072], P(None, 'fsdp'), may hold values from -3 to 3
- down_weight: bfloat16 [2, 3072, 768], P(None, 'fsdp'), may hold values from -0.109375 to 0.109375
- down_bias: bfloat16 [2, 768], P(None, 'fsdp'), may hold values from -1.75 to 1.75
- output_cotangent: bfloat16 [16, 1024, 768], P('fsdp', 'seq'), may hold values from -6 to 6
Outputs:
- layer_output: bfloat16 [16, 1024, 768], P('fsdp', 'seq')
- input_grad: float32 [16, 1024, 768], P('fsdp', 'seq')
- grad_first_gain: float32 [2, 768], P(None, 'fsdp')
- grad_first_shift: float32 [2, 768], P(None, 'fsdp')
- grad_input_weight: float32 [2, 768, 2304], P(None, 'fsdp')
- grad_query_bias: float32 [2, 768], P(None, 'fsdp')
- grad_value_bias: float32 [2, 768], P(None, 'fsdp')
- grad_output_weight: float32 [2, 768, 768], P(None, 'fsdp')
- grad_output_bias: float32 [2, 768], P(None, 'fsdp')
- grad_second_gain: float32 [2, 768], P(None, 'fsdp')
- grad_second_shift: float32 [2, 768], P(None, 'fsdp')
- grad_up_weight: float32 [2, 768, 3072], P(None, 'fsdp')
- grad_up_bias: float32 [2, 3072], P(None, 'fsdp')
- grad_down_weight: float32 [2, 3072, 768], P(None, 'fsdp')
- grad_down_bias: float32 [2, 768], P(None, 'fsdp')
Inputs may be any that keep to these rules, and one draw needn't show every extreme that they name: `segment_ids`: along each packed row the ids never fall; each image holds 1 to 256 tokens and one holds exactly 256.
All inputs are finite; a program needn't handle non-finite values. No bound on the sum of `key_valid` on one device may be relied on, other than what follows from the above.
Results may differ from a plain program's by a relative error of at most 0.015.
Values may be sent and summed in bfloat16 or wider, within the bound.
No kernel may reach another device: no remote copies, remote signals or barrier semaphores. Data moves between devices by JAX's collectives and lax.ppermute only.
A program may use at most 256 MiB of HBM per device.

v0:
```python
import jax
import jax.numpy as jnp
from jax import lax
from jax.sharding import PartitionSpec as P

D = 768
HD = 64
LAYERS = 2


EPS = 1e-06
NEG = -1e30


def layer_norm(values, norm_gain, norm_shift):
    center = values - jnp.mean(values, axis=-1, keepdims=True)
    spread = jnp.mean(center * center, axis=-1, keepdims=True)
    return center * lax.rsqrt(spread + EPS) * norm_gain + norm_shift


def gelu_exact(values):
    return 0.5 * values * (1.0 + lax.erf(values * 2.0 ** (-0.5)))


def outer_sum(left_side, right_side):
    return lax.dot_general(
        left_side, right_side, (((0, 1), (0, 1)), ((), ())), preferred_element_type=jnp.float32
    )


def back_dot(left_side, matrix):
    return lax.dot_general(
        left_side, matrix, (((2,), (1,)), ((), ())), preferred_element_type=jnp.float32
    )


def column_sum(values):
    return jnp.sum(values, axis=(0, 1), dtype=jnp.float32)


def allowed_pairs(segment_row, valid_row):
    places = jnp.arange(segment_row.shape[0])
    return (segment_row[:, None] == segment_row[None, :]) & (
        (valid_row[None, :] == 1) | (places[:, None] == places[None, :])
    )


def masked_scores(queries, keys_in, segment_row, valid_row):
    scores = jnp.einsum(
        "qhd,khd->hqk", queries, keys_in, preferred_element_type=jnp.float32
    ) * HD ** (-0.5)
    return jnp.where(allowed_pairs(segment_row, valid_row)[None], scores, NEG)


def split_heads(row_mix):
    length = row_mix.shape[0]
    local_heads = row_mix.shape[2] // HD
    return (
        row_mix[:, 0].reshape(length, local_heads, HD),
        row_mix[:, 1].reshape(length, local_heads, HD),
        row_mix[:, 2].reshape(length, local_heads, HD),
    )


def attend_forward(packed):
    row_mix, segment_row, valid_row = packed
    length = row_mix.shape[0]
    local_width = row_mix.shape[2]
    queries, keys_in, values_in = split_heads(row_mix)
    scores = masked_scores(queries, keys_in, segment_row, valid_row)
    row_max = jnp.max(scores, axis=-1, keepdims=True)
    expo_terms = jnp.exp(scores - row_max)
    totals = jnp.sum(expo_terms, axis=-1, keepdims=True)
    chances = (expo_terms / totals).astype(jnp.bfloat16)
    attended = jnp.einsum("hqk,khd->qhd", chances, values_in, preferred_element_type=jnp.float32)
    log_totals = row_max[:, :, 0] + jnp.log(totals[:, :, 0])
    return (attended.reshape(length, local_width).astype(jnp.bfloat16), log_totals)


def attend_backward(packed):
    row_mix, log_totals, grad_row, segment_row, valid_row = packed
    length = row_mix.shape[0]
    local_width = row_mix.shape[2]
    queries, keys_in, values_in = split_heads(row_mix)
    grad_heads = grad_row.reshape(length, local_width // HD, HD)
    scores = masked_scores(queries, keys_in, segment_row, valid_row)
    chances = jnp.exp(scores - log_totals[:, :, None])
    grad_chances = jnp.einsum(
        "qhd,khd->hqk", grad_heads, values_in, preferred_element_type=jnp.float32
    )
    inner = jnp.sum(chances * grad_chances, axis=-1, keepdims=True)
    grad_scores = (chances * (grad_chances - inner)).astype(jnp.bfloat16)
    grad_queries = jnp.einsum(
        "hqk,khd->qhd", grad_scores, keys_in, preferred_element_type=jnp.float32
    ) * HD ** (-0.5)
    grad_keys = jnp.einsum(
        "hqk,qhd->khd", grad_scores, queries, preferred_element_type=jnp.float32
    ) * HD ** (-0.5)
    grad_values = jnp.einsum(
        "hqk,qhd->khd", chances.astype(jnp.bfloat16), grad_heads, preferred_element_type=jnp.float32
    )
    stacked = jnp.stack(
        [
            grad_queries.reshape(length, local_width),
            grad_keys.reshape(length, local_width),
            grad_values.reshape(length, local_width),
        ],
        axis=1,
    )
    return stacked.astype(jnp.bfloat16)


def local(
    layer_input,
    segment_ids,
    key_valid,
    first_gain,
    first_shift,
    input_weight,
    query_bias,
    value_bias,
    output_weight,
    output_bias,
    second_gain,
    second_shift,
    up_weight,
    up_bias,
    down_weight,
    down_bias,
    output_cotangent,
):
    row_count = layer_input.shape[0]
    stream = layer_input.astype(jnp.float32)
    kept = []
    for depth_index in range(LAYERS):
        gathered = (
            lax.all_gather(first_gain[depth_index], "fsdp", axis=0, tiled=True),
            lax.all_gather(first_shift[depth_index], "fsdp", axis=0, tiled=True),
            lax.all_gather(input_weight[depth_index], "fsdp", axis=0, tiled=True),
            lax.all_gather(query_bias[depth_index], "fsdp", axis=0, tiled=True),
            lax.all_gather(value_bias[depth_index], "fsdp", axis=0, tiled=True),
            lax.all_gather(output_weight[depth_index], "fsdp", axis=0, tiled=True),
            lax.all_gather(output_bias[depth_index], "fsdp", axis=0, tiled=True),
            lax.all_gather(second_gain[depth_index], "fsdp", axis=0, tiled=True),
            lax.all_gather(second_shift[depth_index], "fsdp", axis=0, tiled=True),
            lax.all_gather(up_weight[depth_index], "fsdp", axis=0, tiled=True),
            lax.all_gather(up_bias[depth_index], "fsdp", axis=0, tiled=True),
            lax.all_gather(down_weight[depth_index], "fsdp", axis=0, tiled=True),
            lax.all_gather(down_bias[depth_index], "fsdp", axis=0, tiled=True),
        )
        (
            gain_one,
            shift_one,
            mix_weight,
            query_shift,
            value_shift,
            out_weight,
            out_shift,
            gain_two,
            shift_two,
            rise_weight,
            rise_shift,
            fall_weight,
            fall_shift,
        ) = gathered
        normed = layer_norm(
            stream, gain_one.astype(jnp.float32), shift_one.astype(jnp.float32)
        ).astype(jnp.bfloat16)
        bias_full = jnp.concatenate(
            [
                query_shift.astype(jnp.float32),
                jnp.zeros((D,), jnp.float32),
                value_shift.astype(jnp.float32),
            ]
        )
        mixed = (
            jnp.dot(normed, mix_weight, preferred_element_type=jnp.float32) + bias_full
        ).astype(jnp.bfloat16)
        mixed = mixed.reshape(row_count, mixed.shape[1], 3, D)
        heads_mix = lax.all_to_all(mixed, "seq", split_axis=3, concat_axis=1, tiled=True)
        attended, log_totals = lax.map(attend_forward, (heads_mix, segment_ids, key_valid))
        attended_tok = lax.all_to_all(attended, "seq", split_axis=1, concat_axis=2, tiled=True)
        stream_mid = stream + (
            jnp.dot(attended_tok, out_weight, preferred_element_type=jnp.float32)
            + out_shift.astype(jnp.float32)
        )
        normed_two = layer_norm(
            stream_mid, gain_two.astype(jnp.float32), shift_two.astype(jnp.float32)
        ).astype(jnp.bfloat16)
        before = jnp.dot(
            normed_two, rise_weight, preferred_element_type=jnp.float32
        ) + rise_shift.astype(jnp.float32)
        hidden = gelu_exact(before).astype(jnp.bfloat16)
        stream_next = stream_mid + (
            jnp.dot(hidden, fall_weight, preferred_element_type=jnp.float32)
            + fall_shift.astype(jnp.float32)
        )
        kept.append(
            (
                stream,
                normed,
                heads_mix,
                log_totals,
                attended_tok,
                stream_mid,
                normed_two,
                before,
                hidden,
                gathered,
            )
        )
        stream = stream_next
    grad_stream = output_cotangent.astype(jnp.float32)
    results = [None] * LAYERS
    for depth_index in reversed(range(LAYERS)):
        (
            stream_in,
            normed,
            heads_mix,
            log_totals,
            attended_tok,
            stream_mid,
            normed_two,
            before,
            hidden,
            gathered,
        ) = kept[depth_index]
        weights_now = (
            lax.all_gather(first_gain[depth_index], "fsdp", axis=0, tiled=True),
            lax.all_gather(first_shift[depth_index], "fsdp", axis=0, tiled=True),
            lax.all_gather(input_weight[depth_index], "fsdp", axis=0, tiled=True),
            lax.all_gather(query_bias[depth_index], "fsdp", axis=0, tiled=True),
            lax.all_gather(value_bias[depth_index], "fsdp", axis=0, tiled=True),
            lax.all_gather(output_weight[depth_index], "fsdp", axis=0, tiled=True),
            lax.all_gather(output_bias[depth_index], "fsdp", axis=0, tiled=True),
            lax.all_gather(second_gain[depth_index], "fsdp", axis=0, tiled=True),
            lax.all_gather(second_shift[depth_index], "fsdp", axis=0, tiled=True),
            lax.all_gather(up_weight[depth_index], "fsdp", axis=0, tiled=True),
            lax.all_gather(up_bias[depth_index], "fsdp", axis=0, tiled=True),
            lax.all_gather(down_weight[depth_index], "fsdp", axis=0, tiled=True),
            lax.all_gather(down_bias[depth_index], "fsdp", axis=0, tiled=True),
        )
        (
            gain_one,
            shift_one,
            mix_weight,
            query_shift,
            value_shift,
            out_weight,
            out_shift,
            gain_two,
            shift_two,
            rise_weight,
            rise_shift,
            fall_weight,
            fall_shift,
        ) = weights_now
        grad_fall = grad_stream.astype(jnp.bfloat16)
        fall_weight_grad = outer_sum(hidden, grad_fall)
        fall_shift_grad = column_sum(grad_fall)
        grad_hidden = back_dot(grad_fall, fall_weight)
        gelu_pair = jax.vjp(gelu_exact, before)
        grad_before = gelu_pair[1](grad_hidden)[0].astype(jnp.bfloat16)
        rise_weight_grad = outer_sum(normed_two, grad_before)
        rise_shift_grad = column_sum(grad_before)
        grad_normed_two = back_dot(grad_before, rise_weight)
        norm_pair_two = jax.vjp(
            layer_norm, stream_mid, gain_two.astype(jnp.float32), shift_two.astype(jnp.float32)
        )
        grad_mid_norm, gain_two_grad, shift_two_grad = norm_pair_two[1](grad_normed_two)
        grad_mid = grad_stream + grad_mid_norm
        grad_branch = grad_mid.astype(jnp.bfloat16)
        out_weight_grad = outer_sum(attended_tok, grad_branch)
        out_shift_grad = column_sum(grad_branch)
        grad_attended = back_dot(grad_branch, out_weight).astype(jnp.bfloat16)
        grad_heads = lax.all_to_all(grad_attended, "seq", split_axis=2, concat_axis=1, tiled=True)
        grad_mix_heads = lax.map(
            attend_backward, (heads_mix, log_totals, grad_heads, segment_ids, key_valid)
        )
        grad_mix = lax.all_to_all(grad_mix_heads, "seq", split_axis=1, concat_axis=3, tiled=True)
        grad_mix = grad_mix.reshape(row_count, grad_mix.shape[1], 3 * D)
        mix_weight_grad = outer_sum(normed, grad_mix)
        mix_sums = column_sum(grad_mix)
        grad_normed = back_dot(grad_mix, mix_weight)
        norm_pair_one = jax.vjp(
            layer_norm, stream_in, gain_one.astype(jnp.float32), shift_one.astype(jnp.float32)
        )
        grad_in_norm, gain_one_grad, shift_one_grad = norm_pair_one[1](grad_normed)
        grad_stream = grad_mid + grad_in_norm
        (
            owned_gain_one,
            owned_shift_one,
            owned_mix_weight,
            owned_query,
            owned_value,
            owned_out_weight,
            owned_out_shift,
            owned_gain_two,
            owned_shift_two,
            owned_rise_weight,
            owned_rise_shift,
            owned_fall_weight,
            owned_fall_shift,
        ) = (
            lax.psum_scatter(gain_one_grad, "fsdp", scatter_dimension=0, tiled=True),
            lax.psum_scatter(shift_one_grad, "fsdp", scatter_dimension=0, tiled=True),
            lax.psum_scatter(mix_weight_grad, "fsdp", scatter_dimension=0, tiled=True),
            lax.psum_scatter(mix_sums[:D], "fsdp", scatter_dimension=0, tiled=True),
            lax.psum_scatter(mix_sums[2 * D :], "fsdp", scatter_dimension=0, tiled=True),
            lax.psum_scatter(out_weight_grad, "fsdp", scatter_dimension=0, tiled=True),
            lax.psum_scatter(out_shift_grad, "fsdp", scatter_dimension=0, tiled=True),
            lax.psum_scatter(gain_two_grad, "fsdp", scatter_dimension=0, tiled=True),
            lax.psum_scatter(shift_two_grad, "fsdp", scatter_dimension=0, tiled=True),
            lax.psum_scatter(rise_weight_grad, "fsdp", scatter_dimension=0, tiled=True),
            lax.psum_scatter(rise_shift_grad, "fsdp", scatter_dimension=0, tiled=True),
            lax.psum_scatter(fall_weight_grad, "fsdp", scatter_dimension=0, tiled=True),
            lax.psum_scatter(fall_shift_grad, "fsdp", scatter_dimension=0, tiled=True),
        )
        results[depth_index] = (
            lax.psum(owned_gain_one.astype(jnp.bfloat16), "seq").astype(jnp.float32),
            lax.psum(owned_shift_one.astype(jnp.bfloat16), "seq").astype(jnp.float32),
            lax.psum(owned_mix_weight.astype(jnp.bfloat16), "seq").astype(jnp.float32),
            lax.psum(owned_query.astype(jnp.bfloat16), "seq").astype(jnp.float32),
            lax.psum(owned_value.astype(jnp.bfloat16), "seq").astype(jnp.float32),
            lax.psum(owned_out_weight.astype(jnp.bfloat16), "seq").astype(jnp.float32),
            lax.psum(owned_out_shift.astype(jnp.bfloat16), "seq").astype(jnp.float32),
            lax.psum(owned_gain_two.astype(jnp.bfloat16), "seq").astype(jnp.float32),
            lax.psum(owned_shift_two.astype(jnp.bfloat16), "seq").astype(jnp.float32),
            lax.psum(owned_rise_weight.astype(jnp.bfloat16), "seq").astype(jnp.float32),
            lax.psum(owned_rise_shift.astype(jnp.bfloat16), "seq").astype(jnp.float32),
            lax.psum(owned_fall_weight.astype(jnp.bfloat16), "seq").astype(jnp.float32),
            lax.psum(owned_fall_shift.astype(jnp.bfloat16), "seq").astype(jnp.float32),
        )
    stacked = [
        jnp.stack([results[depth_index][member] for depth_index in range(LAYERS)])
        for member in range(13)
    ]
    return (
        stream.astype(jnp.bfloat16),
        grad_stream,
        stacked[0],
        stacked[1],
        stacked[2],
        stacked[3],
        stacked[4],
        stacked[5],
        stacked[6],
        stacked[7],
        stacked[8],
        stacked[9],
        stacked[10],
        stacked[11],
        stacked[12],
    )


def solution(mesh):
    placed = (
        P("fsdp", "seq", None),
        P("fsdp", None),
        P("fsdp", None),
        P(None, "fsdp"),
        P(None, "fsdp"),
        P(None, "fsdp", None),
        P(None, "fsdp"),
        P(None, "fsdp"),
        P(None, "fsdp", None),
        P(None, "fsdp"),
        P(None, "fsdp"),
        P(None, "fsdp"),
        P(None, "fsdp", None),
        P(None, "fsdp"),
        P(None, "fsdp", None),
        P(None, "fsdp"),
        P("fsdp", "seq", None),
    )
    return jax.shard_map(
        local,
        mesh=mesh,
        in_specs=placed,
        out_specs=(
            P("fsdp", "seq", None),
            P("fsdp", "seq", None),
            P(None, "fsdp"),
            P(None, "fsdp"),
            P(None, "fsdp", None),
            P(None, "fsdp"),
            P(None, "fsdp"),
            P(None, "fsdp", None),
            P(None, "fsdp"),
            P(None, "fsdp"),
            P(None, "fsdp"),
            P(None, "fsdp", None),
            P(None, "fsdp"),
            P(None, "fsdp", None),
            P(None, "fsdp"),
        ),
        check_vma=False,
    )
```

profile of v0, /device:TPU:0, one launch (start us, length us, event | category | flops | bytes accessed | tf_op | source)
XLA Modules:
  0.0 1397.3 jit_solution(13296752855658942134)
XLA Ops:
  21.0 64.5 %all-reduce.37 = (bf16[768]{0:T(1024)(128)(2,1)S(1)}, bf16[768]{0:T(1024)(128)(2,1)S(1)}, bf16[768]{0:T(1024)(128)(2,1)S(1)}, bf16[768]{0:T(1024)(128)(2,1)S(1)}...) all-reduce(bf16[768]{0:T(1024)(128)(2,1)S(1)} %dynamic-update-slice, ...), channel_id=6, replica_groups=mesh['seq'=2,'fsdp'=16] {'fsdp'}, use_global_device_ids=true, to_apply=%add.3 | all-reduce | flops 18432 | bytes 73728
  109.1 29.8 %all-to-all-done = bf16[1,512,3,768]{1,2,0,3:T(4,128)(2,1)} async-done(((bf16[1,512,3,768]{1,2,0,3:T(4,128)(2,1)}), bf16[1,512,3,768]{1,2,0,3:T(4,128)(2,1)}, u32[]{:S(2)}, u32[]{:S(2)}) %all-to-all-start) | async-done | bytes 2359328 | tf_op jit(solution)/shard_map/all_to_all | solution.py:180
  154.8 10.8 fusion.147
  165.6 10.3 fusion
  175.9 11.4 fusion.71
  237.4 20.5 %all-gather.43.cloned.1.call-done = bf16[1,768,2304]{2,1,0:T(8,128)(2,1)} async-done(((bf16[1,48,2304]{2,1,0:T(8,128)(2,1)}), bf16[1,768,2304]{2,1,0:T(8,128)(2,1)}) %all-gather.43.cloned.1.call-update) | async-done | bytes 3538960 | tf_op jit(solution)/shard_map/all_gather | solution.py:139
  276.4 36.1 %all-to-all-done.2 = bf16[1,512,3,768]{1,2,0,3:T(4,128)(2,1)} async-done(((bf16[1,512,3,768]{1,2,0,3:T(4,128)(2,1)}), bf16[1,512,3,768]{1,2,0,3:T(4,128)(2,1)}, u32[]{:S(2)}, u32[]{:S(2)}) %all-to-all-start.2) | async-done | bytes 2359328 | tf_op jit(solution)/shard_map/all_to_all | solution.py:180
  326.2 10.7 fusion.150
  336.9 10.5 fusion.1
  347.4 10.8 fusion.70
  372.2 10.5 all-to-all-done.3
  391.6 8.5 multiply_convert_fusion.2
  437.3 11.4 all-to-all-done.4
  456.1 11.2 fusion.64
  467.3 16.1 %multiply_reduce_fusion.1 = (f32[6,1024]{1,0:T(8,128)S(1)}, f32[6,1024,1024]{1,2,0:T(8,128)}) fusion(f32[6,1024,1024]{1,2,0:T(8,128)} %get-tuple-element.225, f32[6,1024]{1,0:T(8,128)S(1)} %log_add_fusion.1, bf16[1024,6,64]{0,2,1:T(8,128)(2,1)S(1)} %reshape.725, bf16[1024,6,64]{0,2,1:T(8,128)(2,1)} %bitcast.407), kind=kOutput, calls=%fused_computation.4 | convolution fusion | flops 824174592 | bytes 51953664 | tf_op jit(solution)/shard_map/while/body/eval_jaxpr/qhd,khd->hqk/dot_general | solution.py:88
  483.4 17.0 %multiply_convert_fusion.1 = bf16[6,1024,1024]{1,2,0:T(8,128)(2,1)S(1)} fusion(f32[6,1024,1024]{1,2,0:T(8,128)} %get-tuple-element.232, f32[6,1024,1024]{1,2,0:T(8,128)} %get-tuple-element.225, f32[6,1024]{1,0:T(8,128)S(1)} %get-tuple-element.231, f32[6,1024]{1,0:T(8,128)S(1)} %log_add_fusion.1), kind=kLoop, calls=%fused_computation.3 | loop fusion | flops 25165824 | bytes 62963712 | tf_op jit(solution)/shard_map/while/body/eval_jaxpr/convert_element_type | solution.py:92
  535.2 33.6 %all-to-all-done.5 = bf16[1,1024,3,384]{3,2,0,1:T(4,128)(2,1)} async-done(((bf16[1,1024,3,384]{3,2,0,1:T(4,128)(2,1)}), bf16[1,1024,3,384]{3,2,0,1:T(4,128)(2,1)}, u32[]{:S(2)}, u32[]{:S(2)}) %all-to-all-start.5) | async-done | bytes 2359328 | tf_op jit(solution)/shard_map/all_to_all | solution.py:280
  626.0 9.5 all-to-all-done.6
  642.8 11.3 fusion.67
  658.9 16.2 %multiply_reduce_fusion = (f32[6,1024]{1,0:T(8,128)S(1)}, f32[6,1024,1024]{1,2,0:T(8,128)}) fusion(f32[6,1024,1024]{1,2,0:T(8,128)} %get-tuple-element.217, f32[6,1024]{1,0:T(8,128)S(1)} %log_add_fusion, bf16[1024,6,64]{0,2,1:T(8,128)(2,1)S(1)} %reshape.729, bf16[1024,6,64]{0,2,1:T(8,128)(2,1)} %bitcast.405), kind=kOutput, calls=%fused_computation.1 | convolution fusion | flops 824174592 | bytes 51953664 | tf_op jit(solution)/shard_map/while/body/eval_jaxpr/qhd,khd->hqk/dot_general | solution.py:88
  675.0 20.1 %multiply_convert_fusion = bf16[6,1024,1024]{1,2,0:T(8,128)(2,1)S(1)} fusion(f32[6,1024,1024]{1,2,0:T(8,128)} %get-tuple-element.236, f32[6,1024,1024]{1,2,0:T(8,128)} %get-tuple-element.217, f32[6,1024]{1,0:T(8,128)S(1)} %get-tuple-element.235, f32[6,1024]{1,0:T(8,128)S(1)} %log_add_fusion), kind=kLoop, calls=%fused_computation | loop fusion | flops 25165824 | bytes 62963712 | tf_op jit(solution)/shard_map/while/body/eval_jaxpr/convert_element_type | solution.py:92
  726.2 37.4 %all_to_all.120 = bf16[1,1024,3,384]{3,2,0,1:T(4,128)(2,1)S(1)} all-to-all(bf16[1,1024,3,384]{3,2,0,1:T(4,128)(2,1)S(1)} %pad_maximum_fusion.1), channel_id=1, replica_groups=mesh['seq'=2,'fsdp'=16] {'seq'}, dimensions={1} | all-to-all | bytes 4718592 | tf_op jit(solution)/shard_map/all_to_all | solution.py:280
  776.7 8.8 fusion.92
  786.2 9.5 fusion.124
  796.4 9.0 fusion.130
  805.5 8.4 fusion.86
  841.5 59.7 %all-reduce.36 = (bf16[768]{0:T(1024)(128)(2,1)S(1)}, bf16[768]{0:T(1024)(128)(2,1)S(1)}, bf16[768]{0:T(1024)(128)(2,1)S(1)}, bf16[768]{0:T(1024)(128)(2,1)S(1)}...) all-reduce(f32[768]{0:T(1024)S(1)} %get-tuple-element.90, ...), channel_id=29, replica_groups=mesh['seq'=2,'fsdp'=16] {'fsdp'}, use_global_device_ids=true, to_apply=%region_26.27.clone | all-reduce | flops 18432 | bytes 110592
  908.2 71.5 %reduce-scatter.23.cloned.1.call-done = f32[192,768]{1,0:T(8,128)} async-done(((f32[3072,768]{1,0:T(8,128)}), f32[192,768]{1,0:T(8,128)}) %reduce-scatter.23.cloned.1.call-update) | async-done | bytes 589840 | tf_op jit(solution)/shard_map/reduce_scatter | solution.py:316
  981.6 113.1 %reduce-scatter.19.cloned.1.call-done = f32[48,3072]{1,0:T(8,128)} async-done(((f32[768,3072]{1,0:T(8,128)}), f32[48,3072]{1,0:T(8,128)}) %reduce-scatter.19.cloned.1.call-update) | async-done | bytes 589840 | tf_op jit(solution)/shard_map/reduce_scatter | solution.py:314
  1096.4 113.1 %reduce-scatter.17.cloned.1.call-done = f32[48,3072]{1,0:T(8,128)} async-done(((f32[768,3072]{1,0:T(8,128)}), f32[48,3072]{1,0:T(8,128)}) %reduce-scatter.17.cloned.1.call-update) | async-done | bytes 589840 | tf_op jit(solution)/shard_map/reduce_scatter | solution.py:314
  1211.3 113.0 %reduce-scatter.21.cloned.1.call-done = f32[192,768]{1,0:T(8,128)} async-done(((f32[3072,768]{1,0:T(8,128)}), f32[192,768]{1,0:T(8,128)}) %reduce-scatter.21.cloned.1.call-update) | async-done | bytes 589840 | tf_op jit(solution)/shard_map/reduce_scatter | solution.py:316
  1343.5 40.1 %all-reduce.42.cloned.1.call-done = (bf16[1,48,2304]{2,1,0:T(8,128)(2,1)}, bf16[1,48,2304]{2,1,0:T(8,128)(2,1)}, bf16[1,48,768]{2,1,0:T(8,128)(2,1)}, bf16[1,48,...) async-done(((bf16[1,48,2304]{2,1,0:T(8,128)(2,1)}, ...) | async-done | bytes 1769488 | tf_op jit(solution)/shard_map/psum | solution.py:322
  (483 shorter events, 414.8 us)
Async XLA Ops:
  7.3 78.2 %copy-start.5 = (bf16[1,512,768]{2,1,0:T(8,128)(2,1)S(1)}, bf16[1,512,768]{2,1,0:T(8,128)(2,1)}, u32[]{:S(2)}) copy-start(bf16[1,512,768]{2,1,0:T(8,128)(2,1)} %param.17) | copy-start | bytes 2359300
  7.3 78.8 %all-gather.35.cloned.1.call-start = ((), (), s32[]{:S(2)}) async-start(), calls=%async_computation.24 | async-start | bytes 3760128 | tf_op jit(solution)/shard_map/all_gather | solution.py:139
  9.4 208.7 %all-gather.37.cloned.1.call-start = ((), (), s32[]{:S(2)}) async-start(), calls=%async_computation.25 | async-start | bytes 1253376 | tf_op jit(solution)/shard_map/all_gather | solution.py:142
  11.0 209.9 %all-gather.39.cloned.1.call-start = ((), (), s32[]{:S(2)}) async-start(), calls=%async_computation.26 | async-start | bytes 5013504 | tf_op jit(solution)/shard_map/all_gather | solution.py:146
  13.0 216.3 %all-gather.41.cloned.1.call-start = ((), (), s32[]{:S(2)}) async-start(), calls=%async_computation.27 | async-start | bytes 5013504 | tf_op jit(solution)/shard_map/all_gather | solution.py:148
  13.9 243.9 %all-gather.43.cloned.1.call-start = ((), (), s32[]{:S(2)}) async-start(), calls=%async_computation.28 | async-start | bytes 3760128 | tf_op jit(solution)/shard_map/all_gather | solution.py:139
  14.5 372.6 %all-gather.45.cloned.1.call-start = ((), (), s32[]{:S(2)}) async-start(), calls=%async_computation.29 | async-start | bytes 1253376 | tf_op jit(solution)/shard_map/all_gather | solution.py:142
  101.5 37.4 %all-to-all-start = ((bf16[1,512,3,768]{1,2,0,3:T(4,128)(2,1)}), bf16[1,512,3,768]{1,2,0,3:T(4,128)(2,1)}, u32[]{:S(2)}, u32[]{:S(2)}) async-start(bf16[1,512,3,768]{1,2,0,3:T(4,128)(2,1)} %copy.129), calls=%async_computation | async-start | bytes 6291456 | tf_op jit(solution)/shard_map/all_to_all | solution.py:180
  106.8 284.7 %all-gather.47.cloned.1.call-start = ((), (), s32[]{:S(2)}) async-start(), calls=%async_computation.30 | async-start | bytes 5013504 | tf_op jit(solution)/shard_map/all_gather | solution.py:146
  200.3 12.4 all-to-all-start.1
  204.6 53.2 %copy-start.57 = (f32[768]{0:T(1024)}, f32[768]{0:T(1024)S(1)}, u32[]{:S(2)}) copy-start(f32[768]{0:T(1024)S(1)} %convert_element_type.445) | copy-start | bytes 9220
  204.7 53.2 %copy-start.77 = (f32[768]{0:T(1024)}, f32[768]{0:T(1024)S(1)}, u32[]{:S(2)}) copy-start(f32[768]{0:T(1024)S(1)} %convert_element_type.446) | copy-start | bytes 9220
  235.3 22.5 %copy-start.45 = (f32[512]{0:T(512)}, f32[512]{0:T(512)S(1)}, u32[]{:S(2)}) copy-start(f32[512]{0:T(512)S(1)} %broadcast_multiply_fusion.1) | copy-start | bytes 6148
  237.4 26.6 %copy-start.68 = (f32[512]{0:T(512)}, f32[512]{0:T(512)S(1)}, u32[]{:S(2)}) copy-start(f32[512]{0:T(512)S(1)} %fusion.100) | copy-start | bytes 6148
  270.5 42.0 %all-to-all-start.2 = ((bf16[1,512,3,768]{1,2,0,3:T(4,128)(2,1)}), bf16[1,512,3,768]{1,2,0,3:T(4,128)(2,1)}, u32[]{:S(2)}, u32[]{:S(2)}) async-start(bf16[1,512,3,768]{1,2,0,3:T(4,128)(2,1)} %copy.139), calls=%async_computation.2 | async-start | bytes 6291456 | tf_op jit(solution)/shard_map/all_to_all | solution.py:180
  275.7 130.1 %all-gather.49.cloned.1.call-start = ((), (), s32[]{:S(2)}) async-start(), calls=%async_computation.31 | async-start | bytes 5013504 | tf_op jit(solution)/shard_map/all_gather | solution.py:148
  368.6 14.1 %all-to-all-start.3 = ((bf16[2,2,98304]{2,1,0:T(2,128)(2,1)}), bf16[2,2,98304]{2,1,0:T(2,128)(2,1)S(1)}, u32[]{:S(2)}, u32[]{:S(2)}) async-start(bf16[2,2,98304]{2,1,0:T(2,128)(2,1)} %reshape.924), calls=%async_computation.3 | async-start | bytes 1572864 | tf_op jit(solution)/shard_map/all_to_all | solution.py:182
  372.1 45.5 %copy-start.59 = (f32[768]{0:T(1024)}, f32[768]{0:T(1024)S(1)}, u32[]{:S(2)}) copy-start(f32[768]{0:T(1024)S(1)} %convert_element_type.450) | copy-start | bytes 9220
  390.1 27.6 %copy-start.43 = (f32[512]{0:T(512)}, f32[512]{0:T(512)S(1)}, u32[]{:S(2)}) copy-start(f32[512]{0:T(512)S(1)} %broadcast_multiply_fusion) | copy-start | bytes 6148
  391.5 26.1 %copy-start.66 = (f32[512]{0:T(512)}, f32[512]{0:T(512)S(1)}, u32[]{:S(2)}) copy-start(f32[512]{0:T(512)S(1)} %fusion.101) | copy-start | bytes 6148
  433.7 15.0 %all-to-all-start.4 = ((bf16[2,2,98304]{2,1,0:T(2,128)(2,1)}), bf16[2,2,98304]{2,1,0:T(2,128)(2,1)S(1)}, u32[]{:S(2)}, u32[]{:S(2)}) async-start(bf16[2,2,98304]{2,1,0:T(2,128)(2,1)} %reshape.926), calls=%async_computation.4 | async-start | bytes 1572864 | tf_op jit(solution)/shard_map/all_to_all | solution.py:276
  527.4 41.4 %all-to-all-start.5 = ((bf16[1,1024,3,384]{3,2,0,1:T(4,128)(2,1)}), bf16[1,1024,3,384]{3,2,0,1:T(4,128)(2,1)}, u32[]{:S(2)}, u32[]{:S(2)}) async-start(bf16[1,1024,3,384]{3,2,0,1:T(4,128)(2,1)} %pad_maximum_fusion), calls=%async_computation.5 | async-start | bytes 6291456 | tf_op jit(solution)/shard_map/all_to_all | solution.py:280
  532.8 368.8 %reduce-scatter.15.cloned.1.call-start = ((), (), s32[]{:S(2)}) async-start(), calls=%async_computation.19 | async-start | bytes 2506752 | tf_op jit(solution)/shard_map/reduce_scatter | solution.py:310
  535.1 368.1 %reduce-scatter.13.cloned.1.call-start = ((), (), s32[]{:S(2)}) async-start(), calls=%async_computation.18 | async-start | bytes 2506752 | tf_op jit(solution)/shard_map/reduce_scatter | solution.py:310
  598.8 306.0 %reduce-scatter.11.cloned.1.call-start = ((), (), s32[]{:S(2)}) async-start(), calls=%async_computation.17 | async-start | bytes 7520256 | tf_op jit(solution)/shard_map/reduce_scatter | solution.py:307
  622.1 13.3 all-to-all-start.6
  625.7 280.8 %reduce-scatter.9.cloned.1.call-start = ((), (), s32[]{:S(2)}) async-start(), calls=%async_computation.16 | async-start | bytes 7520256 | tf_op jit(solution)/shard_map/reduce_scatter | solution.py:307
  776.7 203.1 %reduce-scatter.23.cloned.1.call-start = ((), (), s32[]{:S(2)}) async-start(), calls=%async_computation.23 | async-start | bytes 10027008 | tf_op jit(solution)/shard_map/reduce_scatter | solution.py:316
  785.6 309.1 %reduce-scatter.19.cloned.1.call-start = ((), (), s32[]{:S(2)}) async-start(), calls=%async_computation.21 | async-start | bytes 10027008 | tf_op jit(solution)/shard_map/reduce_scatter | solution.py:314
  795.8 413.7 %reduce-scatter.17.cloned.1.call-start = ((), (), s32[]{:S(2)}) async-start(), calls=%async_computation.20 | async-start | bytes 10027008 | tf_op jit(solution)/shard_map/reduce_scatter | solution.py:314
  805.4 518.9 %reduce-scatter.21.cloned.1.call-start = ((), (), s32[]{:S(2)}) async-start(), calls=%async_computation.22 | async-start | bytes 10027008 | tf_op jit(solution)/shard_map/reduce_scatter | solution.py:316
  814.0 569.6 %all-reduce.42.cloned.1.call-start = ((), (), s32[]{:S(2)}) async-start(), calls=%async_computation.32 | async-start | bytes 3538944 | tf_op jit(solution)/shard_map/psum | solution.py:322
  (93 other events, 587.0 us)
Sparse Core Ops, SparseCore 0:
  11.0 50.4 all-gather.34
  63.8 36.8 all-gather.36
  103.6 51.9 all-gather.38
  158.3 51.6 all-gather.40
  212.1 45.6 all-gather.42
  260.0 36.8 all-gather.44
  299.8 51.9 all-gather.46
  354.1 51.6 all-gather.48
  537.4 62.3 reduce-scatter.14
  603.4 62.2 reduce-scatter.12
  669.7 88.9 reduce-scatter.10
  776.8 87.8 reduce-scatter.8
  868.8 110.9 reduce-scatter.22
  983.7 110.8 reduce-scatter.18
  1098.6 110.8 reduce-scatter.16
  1213.4 110.8 reduce-scatter.20
  1328.0 55.5 all-reduce.41
where the time goes:
time: 1410 us; the launch traced here: 1400 us
  waiting for transfers between devices  618 us (44%)
  matrix products  260 us (18%)
  blocking collectives  170 us (12%)
  local copies, waits for them, and re-layouts  151 us (11%)
  other arithmetic  147 us (10%)
  starting transfers between devices  32.9 us (2%)
  between operations  18.4 us (1%)
    reduce_scatter x2, waiting for transfers between devices, local(): lax.psum_scatter(rise_weight_grad, 'fsdp', scatter_dimension=0, tiled=True)  226 us
    reduce_scatter x2, waiting for transfers between devices, local(): lax.psum_scatter(fall_weight_grad, 'fsdp', scatter_dimension=0, tiled=True)  185 us
    unnamed x2, blocking collectives  124 us
    all_to_all x2, waiting for transfers between devices, local(): lax.all_to_all(mixed, 'seq', split_axis=3, concat_axis=1, tiled=True)  65.9 us
    dot_general x8, matrix products, outer_sum(): lax.dot_general(left_side, right_side, (((0, 1), (0, 1)), ((), ())), pref...  54.2 us
    psum x1, waiting for transfers between devices, local(): lax.psum(owned_mix_weight.astype(jnp.bfloat16), 'seq').astype(jnp.float32)  40.1 us
    dot_general x8, matrix products, back_dot(): lax.dot_general(left_side, matrix, (((2,), (1,)), ((), ())), preferred_el...  38.3 us
    all_to_all x1, blocking collectives, local(): lax.all_to_all(grad_mix_heads, 'seq', split_axis=1, concat_axis=3, tiled=...  37.4 us
  transfers between devices with their start and end apart: 24, of which 14 were waited for; matrix products, arithmetic and copies ran while one was open for 31% of the time, Pallas kernels for 0%

commit v1 on v0

v1 whole, which is shorter than its diff:
```python
import jax
import jax.numpy as jnp
from jax import lax
from jax.experimental import pallas as pl
from jax.experimental.pallas import tpu as pltpu
from jax.sharding import PartitionSpec as P

D = 768
HD = 64
FF = 3072
LAYERS = 2
PAIR = 128
PAIRS = D // PAIR
HALF = 256

EPS = 1e-06
NEG = -1e30
F32 = jnp.float32
BF16 = jnp.bfloat16


def layer_norm(values, norm_gain, norm_shift):
    center = values - jnp.mean(values, axis=-1, keepdims=True)
    spread = jnp.mean(center * center, axis=-1, keepdims=True)
    return center * lax.rsqrt(spread + EPS) * norm_gain + norm_shift


def gelu_exact(values):
    return 0.5 * values * (1.0 + lax.erf(values * 2.0 ** (-0.5)))


def gelu_slope(values):
    return 0.5 * (1.0 + lax.erf(values * 2.0 ** (-0.5))) + values * (
        jnp.exp(-0.5 * values * values) * (2.0 * jnp.pi) ** (-0.5)
    )


def dot(left_side, right_side):
    return jnp.dot(left_side, right_side, preferred_element_type=F32)


def dot_rows(left_side, right_side):
    return lax.dot_general(left_side, right_side, (((0,), (0,)), ((), ())), preferred_element_type=F32)


def dot_back(left_side, right_side):
    return lax.dot_general(left_side, right_side, (((1,), (1,)), ((), ())), preferred_element_type=F32)


def column_sum(values):
    return dot(jnp.ones((8, values.shape[0]), BF16), values)[0]


def attend_kernel(seg_col, seg_row, valid_row, q_ref, kv_ref, halo_ref, out_ref, lse_ref, bias):
    @pl.when(pl.program_id(0) == 0)
    def _():
        rows = lax.broadcasted_iota(jnp.int32, bias.shape, 0)
        columns = lax.broadcasted_iota(jnp.int32, bias.shape, 1)
        allowed = (seg_col[...] == seg_row[...]) & ((valid_row[...] == 1) | (rows == columns))
        bias[...] = jnp.where(allowed, 0.0, NEG)

    lane = lax.broadcasted_iota(jnp.int32, (HALF, PAIR), 1)
    keys, values = kv_ref[:, :PAIR], kv_ref[:, PAIR:]
    halo_keys, halo_values = halo_ref[:, :PAIR], halo_ref[:, PAIR:]
    for block in range(2):
        rows = slice(block * HALF, (block + 1) * HALF)
        queries = q_ref[rows, :] * jnp.asarray(HD ** (-0.5), BF16)
        merged = None
        for head in range(2):
            mine = (lane // HD) == head
            query = jnp.where(mine, queries, jnp.zeros_like(queries))
            scores = dot_back(query, keys) + bias[rows, : 2 * HALF]
            top = jnp.max(scores, axis=1, keepdims=True)
            if block == 0:
                halo_scores = dot_back(query, halo_keys) + bias[rows, 2 * HALF :]
                top = jnp.maximum(top, jnp.max(halo_scores, axis=1, keepdims=True))
            terms = jnp.exp(scores - top)
            total = jnp.sum(terms, axis=1, keepdims=True)
            found = dot(terms.astype(BF16), values)
            if block == 0:
                halo_terms = jnp.exp(halo_scores - top)
                total = total + jnp.sum(halo_terms, axis=1, keepdims=True)
                found = found + dot(halo_terms.astype(BF16), halo_values)
            found = found * (1.0 / total)
            merged = found if merged is None else jnp.where(mine, found, merged)
            lse = jnp.broadcast_to(top + jnp.log(total), (HALF, PAIR))
            lse_ref[0, head : head + 1, rows] = lse.T[:1, :]
        out_ref[rows, :] = merged.astype(BF16)


def attend(segment, valid, queries, pairs, halo_pairs):
    rows, reach = queries.shape[0], segment.shape[0]
    whole = lambda shape: pl.BlockSpec(shape, lambda i: (0, 0))
    return pl.pallas_call(
        attend_kernel,
        grid=(PAIRS,),
        in_specs=[
            whole((rows, 1)),
            whole((1, reach)),
            whole((1, reach)),
            pl.BlockSpec((rows, PAIR), lambda i: (0, i)),
            pl.BlockSpec((rows, 2 * PAIR), lambda i: (0, i)),
            pl.BlockSpec((HALF, 2 * PAIR), lambda i: (0, i)),
        ],
        out_specs=[
            pl.BlockSpec((rows, PAIR), lambda i: (0, i)),
            pl.BlockSpec((1, 2, rows), lambda i: (i, 0, 0)),
        ],
        out_shape=[
            jax.ShapeDtypeStruct((rows, D), BF16),
            jax.ShapeDtypeStruct((PAIRS, 2, rows), F32),
        ],
        scratch_shapes=[pltpu.VMEM((rows, reach), F32)],
        cost_estimate=pl.CostEstimate(flops=4 * 5 * 65536 * D, bytes_accessed=6 << 20, transcendentals=5 * 65536 * 12),
        name="attend",
    )(segment[:rows, None], segment[None, :], valid[None, :], queries, pairs, halo_pairs)


def attend_back_kernel(
    seg_row, seg_col, valid_col, q_ref, kv_ref, halo_ref, grad_ref, lse_ref, dq_ref, dkv_ref, dhalo_ref, bias
):
    @pl.when(pl.program_id(0) == 0)
    def _():
        rows = lax.broadcasted_iota(jnp.int32, bias.shape, 0)
        columns = lax.broadcasted_iota(jnp.int32, bias.shape, 1)
        allowed = (seg_col[...] == seg_row[...]) & ((valid_col[...] == 1) | (rows == columns))
        bias[...] = jnp.where(allowed, 0.0, NEG)

    lane = lax.broadcasted_iota(jnp.int32, (HALF, PAIR), 1)
    keys, values = kv_ref[:, :PAIR], kv_ref[:, PAIR:]
    halo_keys, halo_values = halo_ref[:, :PAIR], halo_ref[:, PAIR:]
    keys_t, halo_keys_t = keys.T, halo_keys.T
    scale = jnp.asarray(HD ** (-0.5), BF16)
    dk = dv = dk_halo = dv_halo = None
    plus = lambda total, term: term if total is None else total + term
    for block in range(2):
        rows = slice(block * HALF, (block + 1) * HALF)
        queries = q_ref[rows, :] * scale
        grads = grad_ref[rows, :]
        dq_parts = []
        for head in range(2):
            mine = (lane // HD) == head
            query = jnp.where(mine, queries, jnp.zeros_like(queries))
            grad = jnp.where(mine, grads, jnp.zeros_like(grads))
            lse = lse_ref[0, head : head + 1, rows]
            dims = slice(head * HD, (head + 1) * HD)
            chances = jnp.exp(dot_back(keys, query) + bias[: 2 * HALF, rows] - lse)
            back = dot_back(values, grad)
            inner = jnp.sum(chances * back, axis=0, keepdims=True)
            if block == 0:
                halo_chances = jnp.exp(dot_back(halo_keys, query) + bias[2 * HALF :, rows] - lse)
                halo_back = dot_back(halo_values, grad)
                inner = inner + jnp.sum(halo_chances * halo_back, axis=0, keepdims=True)
            slopes = (chances * (back - inner)).astype(BF16)
            dq = dot(keys_t[dims, :], slopes)
            dk = plus(dk, dot(slopes, query))
            dv = plus(dv, dot(chances.astype(BF16), grad))
            if block == 0:
                halo_slopes = (halo_chances * (halo_back - inner)).astype(BF16)
                dq = dq + dot(halo_keys_t[dims, :], halo_slopes)
                dk_halo = plus(dk_halo, dot(halo_slopes, query))
                dv_halo = plus(dv_halo, dot(halo_chances.astype(BF16), grad))
            dq_parts.append(dq)
        dq = jnp.concatenate(dq_parts, axis=0).T * HD ** (-0.5)
        dq_ref[rows, :] = dq.astype(BF16)
    dkv_ref[:, :PAIR] = dk.astype(BF16)
    dkv_ref[:, PAIR:] = dv.astype(BF16)
    dhalo_ref[:, :PAIR] = dk_halo.astype(BF16)
    dhalo_ref[:, PAIR:] = dv_halo.astype(BF16)


def attend_back(segment, valid, queries, pairs, halo_pairs, grads, lse):
    rows, reach = queries.shape[0], segment.shape[0]
    whole = lambda shape: pl.BlockSpec(shape, lambda i: (0, 0))
    tokens = pl.BlockSpec((rows, PAIR), lambda i: (0, i))
    both = pl.BlockSpec((rows, 2 * PAIR), lambda i: (0, i))
    halo = pl.BlockSpec((HALF, 2 * PAIR), lambda i: (0, i))
    return pl.pallas_call(
        attend_back_kernel,
        grid=(PAIRS,),
        in_specs=[
            whole((1, rows)),
            whole((reach, 1)),
            whole((reach, 1)),
            tokens,
            both,
            halo,
            tokens,
            pl.BlockSpec((1, 2, rows), lambda i: (i, 0, 0)),
        ],
        out_specs=[tokens, both, halo],
        out_shape=[
            jax.ShapeDtypeStruct((rows, D), BF16),
            jax.ShapeDtypeStruct((rows, 2 * D), BF16),
            jax.ShapeDtypeStruct((HALF, 2 * D), BF16),
        ],
        scratch_shapes=[pltpu.VMEM((reach, rows), F32)],
        cost_estimate=pl.CostEstimate(flops=10 * 5 * 65536 * D, bytes_accessed=10 << 20, transcendentals=5 * 65536 * 12),
        name="attend_back",
    )(segment[None, :rows], segment[:, None], valid[:, None], queries, pairs, halo_pairs, grads, lse)


def swap_seq(values):
    return lax.ppermute(values, "seq", [(0, 1), (1, 0)])


def pair_columns(matrix):
    return matrix.reshape(-1, 2, PAIRS, PAIR).swapaxes(1, 2).reshape(-1, 2 * D)


def unpair_columns(matrix):
    return matrix.reshape(-1, PAIRS, 2, PAIR).swapaxes(1, 2).reshape(-1, 2 * D)


def column_blocks(matrix):
    rows = matrix.shape[0]
    return matrix.reshape(rows, -1, D).swapaxes(0, 1).reshape(-1, D)


def local(
    layer_input,
    segment_ids,
    key_valid,
    first_gain,
    first_shift,
    input_weight,
    query_bias,
    value_bias,
    output_weight,
    output_bias,
    second_gain,
    second_shift,
    up_weight,
    up_bias,
    down_weight,
    down_bias,
    output_cotangent,
):
    right = lax.axis_index("seq") == 1
    rows_of = input_weight.shape[1]
    owners = D // rows_of

    def near_first(values):
        turned = jnp.concatenate([values[HALF:], values[:HALF]], axis=0)
        return jnp.where(right, values, turned)

    def by_block(values):
        blocks = values.reshape(4, HALF)
        return jnp.where(
            right,
            jnp.concatenate([blocks[2], blocks[3], blocks[1]]),
            jnp.concatenate([blocks[1], blocks[0], blocks[2]]),
        )

    def gather(shard):
        return lax.all_gather(shard, "fsdp", axis=0, tiled=False)

    segment, valid = by_block(segment_ids[0]), by_block(key_valid[0])

    ordered = [
        jnp.concatenate([input_weight[depth][:, :D], pair_columns(input_weight[depth][:, D:])], axis=1)
        for depth in range(LAYERS)
    ]
    smalls = [first_gain, first_shift, query_bias, value_bias, output_bias, second_gain, second_shift, down_bias]
    small = jnp.concatenate(
        [member.reshape(LAYERS, 1, rows_of) for member in smalls] + [up_bias.reshape(LAYERS, 4, rows_of)], axis=1
    ).reshape(-1)
    side = rows_of * 128
    small_block = jnp.pad(small, (0, side - small.shape[0])).reshape(rows_of, 128)
    first = gather(jnp.concatenate([ordered[0], small_block], axis=1))

    def rest(depth):
        return [output_weight[depth], column_blocks(up_weight[depth]), down_weight[depth]]

    second = gather(jnp.concatenate(rest(0) + [column_blocks(ordered[1])], axis=0))
    third = gather(jnp.concatenate(rest(1), axis=0))

    def take(packed, start, count):
        part = packed[:, start * rows_of : (start + count) * rows_of]
        return part

    def joined(packed, start, count):
        return jnp.concatenate(
            [take(packed, start + j, 1).reshape(D, D) for j in range(count)], axis=1
        )

    def unpacked(packed):
        return take(packed, 0, 1).reshape(D, D), joined(packed, 1, 4), take(packed, 5, 4).reshape(FF, D)

    first = first.reshape(D, -1)
    mix_weights = [first[:, : 3 * D], joined(second, 9, 3)]
    mlp_weights = [unpacked(second), unpacked(third)]
    smalls_full = (
        first[:, 3 * D :].reshape(owners, side)[:, : small.shape[0]].reshape(owners, LAYERS, 12, rows_of).astype(F32)
    )
    vectors = smalls_full[:, :, :8].transpose(1, 2, 0, 3).reshape(LAYERS, 8, D)
    up_biases = smalls_full[:, :, 8:].transpose(1, 0, 2, 3).reshape(LAYERS, FF)

    stream = near_first(layer_input[0]).astype(F32)
    kept = []
    for depth in range(LAYERS):
        gain_one, shift_one, query_shift, value_shift, out_shift, gain_two, shift_two, fall_shift = [
            vectors[depth, j] for j in range(8)
        ]
        mix_weight = mix_weights[depth]
        out_weight, rise_weight, fall_weight = mlp_weights[depth]
        normed = layer_norm(stream, gain_one, shift_one).astype(BF16)
        halo_normed = swap_seq(normed[:HALF])
        pair_shift = jnp.stack([jnp.zeros((PAIRS, PAIR), F32), value_shift.reshape(PAIRS, PAIR)], axis=1).reshape(-1)
        queries = (dot(normed, mix_weight[:, :D]) + query_shift).astype(BF16)
        pairs = (dot(normed, mix_weight[:, D:]) + pair_shift).astype(BF16)
        halo_pairs = (dot(halo_normed, mix_weight[:, D:]) + pair_shift).astype(BF16)
        attended, lse = attend(segment, valid, queries, pairs, halo_pairs)
        stream_mid = stream + (dot(attended, out_weight) + out_shift)
        normed_two = layer_norm(stream_mid, gain_two, shift_two).astype(BF16)
        before = dot(normed_two, rise_weight) + up_biases[depth]
        hidden = gelu_exact(before).astype(BF16)
        stream_next = stream_mid + (dot(hidden, fall_weight) + fall_shift)
        kept.append((stream, normed, halo_normed, queries, pairs, halo_pairs, lse, attended, stream_mid, normed_two, before, hidden))
        stream = stream_next

    grad_stream = near_first(output_cotangent[0]).astype(F32)
    packs = {}
    small_grads = [None] * LAYERS

    def owned_rows(matrix):
        return matrix.astype(BF16).reshape(owners, -1, D)

    def owned_blocks(matrix):
        blocks = matrix.astype(BF16).reshape(owners, rows_of, -1, D)
        return blocks.swapaxes(1, 2).reshape(owners, -1, D)

    for depth in reversed(range(LAYERS)):
        gain_one, shift_one, query_shift, value_shift, out_shift, gain_two, shift_two, fall_shift = [
            vectors[depth, j] for j in range(8)
        ]
        mix_weight = mix_weights[depth]
        out_weight, rise_weight, fall_weight = mlp_weights[depth]
        (stream_in, normed, halo_normed, queries, pairs, halo_pairs, lse, attended, stream_mid, normed_two, before, hidden) = kept[depth]
        grad_fall = grad_stream.astype(BF16)
        fall_weight_grad = dot_rows(hidden, grad_fall)
        fall_shift_grad = column_sum(grad_fall)
        grad_before = (dot_back(grad_fall, fall_weight) * gelu_slope(before)).astype(BF16)
        rise_weight_grad = dot_rows(normed_two, grad_before)
        rise_shift_grad = column_sum(grad_before)
        grad_normed_two = dot_back(grad_before, rise_weight)
        norm_pair_two = jax.vjp(layer_norm, stream_mid, gain_two, shift_two)
        grad_mid_norm, gain_two_grad, shift_two_grad = norm_pair_two[1](grad_normed_two)
        grad_mid = grad_stream + grad_mid_norm
        grad_branch = grad_mid.astype(BF16)
        out_weight_grad = dot_rows(attended, grad_branch)
        out_shift_grad = column_sum(grad_branch)
        grad_attended = dot_back(grad_branch, out_weight).astype(BF16)
        dq, dpairs, dhalo = attend_back(segment, valid, queries, pairs, halo_pairs, grad_attended, lse)
        halo_back = swap_seq(dot_back(dhalo, mix_weight[:, D:]).astype(BF16)).astype(F32)
        normed_all = jnp.concatenate([normed, halo_normed], axis=0)
        dpairs_all = jnp.concatenate([dpairs, dhalo], axis=0)
        query_weight_grad = dot_rows(normed, dq)
        pair_weight_grad = dot_rows(normed_all, dpairs_all)
        query_shift_grad = column_sum(dq)
        value_shift_grad = column_sum(dpairs_all).reshape(PAIRS, 2, PAIR)[:, 1].reshape(D)
        grad_normed = dot_back(dq, mix_weight[:, :D]) + dot_back(dpairs, mix_weight[:, D:])
        grad_normed = jnp.concatenate([grad_normed[:HALF] + halo_back, grad_normed[HALF:]], axis=0)
        norm_pair_one = jax.vjp(layer_norm, stream_in, gain_one, shift_one)
        grad_in_norm, gain_one_grad, shift_one_grad = norm_pair_one[1](grad_normed)
        grad_stream = grad_mid + grad_in_norm
        packs["fall", depth] = owned_rows(fall_weight_grad)
        packs["rise", depth] = owned_blocks(rise_weight_grad)
        packs["out", depth] = owned_rows(out_weight_grad)
        packs["query", depth] = owned_rows(query_weight_grad)
        packs["pair", depth] = owned_blocks(pair_weight_grad)
        small_grads[depth] = jnp.concatenate(
            [
                member.reshape(owners, 1, rows_of)
                for member in (
                    gain_one_grad,
                    shift_one_grad,
                    query_shift_grad,
                    value_shift_grad,
                    out_shift_grad,
                    gain_two_grad,
                    shift_two_grad,
                    fall_shift_grad,
                )
            ]
            + [rise_shift_grad.reshape(owners, 4, rows_of)],
            axis=1,
        )

    small_all = jnp.concatenate(small_grads, axis=1).astype(BF16).reshape(owners, -1)
    small_all = jnp.pad(small_all, ((0, 0), (0, 16 * D - small_all.shape[1]))).reshape(owners, 16, D)

    def reduced(names):
        parts = [packs[name] for name in names]
        mine = lax.psum_scatter(jnp.concatenate(parts, axis=1), "fsdp", scatter_dimension=0, tiled=False)
        total = mine.astype(F32) + swap_seq(mine).astype(F32)
        found, at = {}, 0
        for name, part in zip(names, parts):
            found[name] = total[at : at + part.shape[1]]
            at += part.shape[1]
        return found

    packs["small", 0] = small_all
    sums = reduced([("fall", 1), ("rise", 1)])
    sums.update(reduced([("out", 1), ("query", 1), ("pair", 1), ("fall", 0), ("rise", 0)]))
    sums.update(reduced([("out", 0), ("query", 0), ("pair", 0), ("small", 0)]))

    def columns(block_rows, count):
        return block_rows.reshape(count, rows_of, D).swapaxes(0, 1).reshape(rows_of, count * D)

    def both(fn):
        return jnp.stack([fn(depth) for depth in range(LAYERS)])

    small_sum = sums["small", 0].reshape(-1)[: small.shape[0]].reshape(LAYERS, 12, rows_of)
    mix_out = both(
        lambda depth: jnp.concatenate(
            [sums["query", depth], unpair_columns(columns(sums["pair", depth], 2))], axis=1
        )
    )
    layer_output = near_first(stream.astype(BF16))[None]
    input_grad = near_first(grad_stream)[None]
    return (
        layer_output,
        input_grad,
        small_sum[:, 0],
        small_sum[:, 1],
        mix_out,
        small_sum[:, 2],
        small_sum[:, 3],
        both(lambda depth: sums["out", depth]),
        small_sum[:, 4],
        small_sum[:, 5],
        small_sum[:, 6],
        both(lambda depth: columns(sums["rise", depth], 4)),
        small_sum[:, 8:].reshape(LAYERS, 4 * rows_of),
        both(lambda depth: sums["fall", depth]),
        small_sum[:, 7],
    )


def solution(mesh):
    vector, matrix = P(None, "fsdp"), P(None, "fsdp", None)
    tokens, places = P("fsdp", "seq", None), P("fsdp", None)
    return jax.shard_map(
        local,
        mesh=mesh,
        in_specs=(
            tokens,
            places,
            places,
            vector,
            vector,
            matrix,
            vector,
            vector,
            matrix,
            vector,
            vector,
            vector,
            matrix,
            vector,
            matrix,
            vector,
            tokens,
        ),
        out_specs=(
            tokens,
            tokens,
            vector,
            vector,
            matrix,
            vector,
            vector,
            matrix,
            vector,
            vector,
            vector,
            matrix,
            vector,
            matrix,
            vector,
        ),
        check_vma=False,
    )
```

time: 1410 us -> 869 us (0.62)
  blocking collectives: 170 us -> 0 us
  waiting for transfers between devices: 618 us -> 472 us
  matrix products: 260 us -> 117 us
  other arithmetic: 147 us -> 33.4 us
  Pallas kernels: 0 us -> 65.2 us
  starting transfers between devices: 32.9 us -> 10 us
    all_gather x8 -> x3, waiting for transfers between devices: 26.3 us -> 201 us  [gather(): return lax.all_gather(shard, 'fsdp', axis=0, tiled=False)]
    reduce_scatter x8 -> x3, waiting for transfers between devices: 411 us -> 239 us  [reduced(): lax.psum_scatter(jnp.concatenate(parts, axis=1), 'fsdp', scatter_dimensio...]
    dot_general x36 -> x44, matrix products: 260 us -> 117 us  [the longest x22 42.9 us: dot(): return jnp.dot(left_side, right_side, preferred_element_type=F32)]
    all_to_all x7 -> x0, waiting for transfers between devices: 139 us -> none  [the longest x2 65.9 us: local(): lax.all_to_all(mixed, 'seq', split_axis=3, concat_axis=1, tiled=True)]
    unnamed x2 -> x0, blocking collectives: 124 us -> none
    pallas_call x0 -> x4, Pallas kernels: none -> 65.2 us  [the longest x2 38.3 us: attend_back(): pl.pallas_call(attend_back_kernel, grid=(PAIRS,), in_specs=[whole((1, row...]
    psum x1 -> x0, waiting for transfers between devices: 40.1 us -> none  [local(): lax.psum(owned_mix_weight.astype(jnp.bfloat16), 'seq').astype(jnp.float32)]
    all_to_all x1 -> x0, blocking collectives: 37.4 us -> none  [local(): lax.all_to_all(grad_mix_heads, 'seq', split_axis=1, concat_axis=3, tiled=...]
  transfers between devices with their start and end apart: 24 -> 13, of which waited for: 14 -> 9; matrix products, arithmetic and copies ran while one was open for 31% -> 20% of each run, Pallas kernels for 0% -> 2%
where the time goes in v1:
time: 869 us; the launch traced here: 861 us
  waiting for transfers between devices  472 us (54%)
  local copies, waits for them, and re-layouts  147 us (17%)
  matrix products  117 us (13%)
  Pallas kernels  65.2 us (8%)
  other arithmetic  33.4 us (4%)
  between operations  16.4 us (2%)
  starting transfers between devices  10 us (1%)
    reduce_scatter x3, waiting for transfers between devices, reduced(): lax.psum_scatter(jnp.concatenate(parts, axis=1), 'fsdp', scatter_dimensio...  239 us
    all_gather x3, waiting for transfers between devices, gather(): return lax.all_gather(shard, 'fsdp', axis=0, tiled=False)  201 us
    dot_general x22, matrix products, dot(): return jnp.dot(left_side, right_side, preferred_element_type=F32)  42.9 us
    dot_general x12, matrix products, dot_back(): lax.dot_general(left_side, right_side, (((1,), (1,)), ((), ())), preferre...  40.2 us
    pallas_call x2, Pallas kernels, attend_back(): pl.pallas_call(attend_back_kernel, grid=(PAIRS,), in_specs=[whole((1, row...  38.3 us
    dot_general x10, matrix products, dot_rows(): lax.dot_general(left_side, right_side, (((0,), (0,)), ((), ())), preferre...  33.8 us
    ppermute x7, waiting for transfers between devices, swap_seq(): return lax.ppermute(values, 'seq', [(0, 1), (1, 0)])  32 us
    reshape x4, local copies, waits for them, and re-layouts, owned_blocks(): blocks = matrix.astype(BF16).reshape(owners, rows_of, -1, D)  31.8 us
  transfers between devices with their start and end apart: 13, of which 9 were waited for; matrix products, arithmetic and copies ran while one was open for 20% of the time, Pallas kernels for 2%

profile of v1, /device:TPU:0, one launch (start us, length us, event | category | flops | bytes accessed | tf_op | source)
XLA Modules:
  0.0 861.2 jit_solution(2057251023151137355)
XLA Ops:
  26.2 40.4 %all-gather.7.cloned.1.call-done = bf16[768,2432]{1,0:T(8,128)(2,1)} async-done(((bf16[48,2432]{1,0:T(8,128)(2,1)}), bf16[768,2432]{1,0:T(8,128)(2,1)}) %all-gather.7.cloned.1.call-update) | async-done | bytes 3735568 | tf_op jit(solution)/shard_map/all_gather | solution.py:256
  77.7 4.1 collective-permute-done
  83.6 13.6 %attend.2 = (bf16[512,768]{1,0:T(8,128)(2,1)}, f32[6,2,512]{2,1,0:T(2,128)}) custom-call(s32[512,1]{1,0:T(8,128)} %copy.182.seg_col, s32[1,768]{1,0:T(1,128)} %get-tuple-element.166.seg_row, s32[1,768]{1,0:T(1,128)} %get-tuple-element.165.valid_row, bf16[512,768]{1,0:T(8,128)(2,1)} %add_convert_fusion.5.q_ref, bf16[512,1536]{1,0:T(8,128)(2,1)} %fusion.12.kv_ref, ...), custom_call_target="tpu_custom_call" | custom-call | flops 1006632960 | bytes 6291456 | tf_op jit(solution)/shard_map/attend/pallas_call | solution.py:94
  97.2 59.3 %all-gather.11.cloned.1.call-done = bf16[6912,768]{1,0:T(8,128)(2,1)} async-done(((bf16[432,768]{1,0:T(8,128)(2,1)}), bf16[6912,768]{1,0:T(8,128)(2,1)}) %all-gather.11.cloned.1.call-update) | async-done | bytes 10616848 | tf_op jit(solution)/shard_map/all_gather | solution.py:256
  156.5 4.9 slice.542
  161.3 5.4 fusion.119
  166.7 101.0 %all-gather.9.cloned.1.call-done = bf16[9216,768]{1,0:T(8,128)(2,1)} async-done(((bf16[576,768]{1,0:T(8,128)(2,1)}), bf16[9216,768]{1,0:T(8,128)(2,1)}) %all-gather.9.cloned.1.call-update) | async-done | bytes 14155792 | tf_op jit(solution)/shard_map/all_gather | solution.py:256
  270.5 5.9 fusion.118
  278.8 5.5 multiply_convert_fusion.1
  294.0 5.6 collective-permute-done.1
  302.1 13.3 %attend.3 = (bf16[512,768]{1,0:T(8,128)(2,1)}, f32[6,2,512]{2,1,0:T(2,128)}) custom-call(s32[512,1]{1,0:T(8,128)} %copy.182.seg_col, s32[1,768]{1,0:T(1,128)} %get-tuple-element.166.seg_row, s32[1,768]{1,0:T(1,128)} %get-tuple-element.165.valid_row, bf16[512,768]{1,0:T(8,128)(2,1)} %add_convert_fusion.2.q_ref, bf16[512,1536]{1,0:T(8,128)(2,1)} %fusion.13.kv_ref, ...), custom_call_target="tpu_custom_call" | custom-call | flops 1006632960 | bytes 6291456 | tf_op jit(solution)/shard_map/attend/pallas_call | solution.py:94
  319.8 6.3 multiply_convert_fusion
  326.2 7.0 fusion.5
  342.3 19.2 %attend_back.2 = (bf16[512,768]{1,0:T(8,128)(2,1)}, bf16[512,1536]{1,0:T(8,128)(2,1)}, bf16[256,1536]{1,0:T(8,128)(2,1)}) custom-call(s32[1,512]{1,0:T(1,128)} %bitcast.305, s32[768,1]{1,0:T(8,128)} %get-tuple-element.164.seg_col, s32[768,1]{1,0:T(8,128)} %get-tuple-element.163.valid_col, bf16[512,768]{1,0:T(8,128)(2,1)} %add_convert_fusion.2.q_ref, ...), custom_call_target="tpu_custom_call" | custom-call | flops 2516582400 | bytes 10485760 | tf_op jit(solution)/shard_map/attend_back/pallas_call | solution.py:178
  361.4 4.8 fusion.111
  395.5 5.1 fusion.11
  411.7 19.1 %attend_back.3 = (bf16[512,768]{1,0:T(8,128)(2,1)}, bf16[512,1536]{1,0:T(8,128)(2,1)}, bf16[256,1536]{1,0:T(8,128)(2,1)}) custom-call(s32[1,512]{1,0:T(1,128)} %bitcast.306, s32[768,1]{1,0:T(8,128)} %get-tuple-element.164.seg_col, s32[768,1]{1,0:T(8,128)} %get-tuple-element.163.valid_col, bf16[512,768]{1,0:T(8,128)(2,1)} %add_convert_fusion.5.q_ref, ...), custom_call_target="tpu_custom_call" | custom-call | flops 2516582400 | bytes 10485760 | tf_op jit(solution)/shard_map/attend_back/pallas_call | solution.py:178
  460.7 6.1 reshape.792
  466.9 3.5 copy.193
  478.8 5.0 pad_maximum_fusion.1
  484.5 7.4 convolution_convert_fusion
  491.9 9.9 %reshape.816 = bf16[16,48,4,768]{3,2,1,0:T(4,128)(2,1)} reshape(bf16[768,3072]{1,0:T(8,128)(2,1)} %convolution_convert_fusion) | data formatting | bytes 9437184 | tf_op jit(solution)/shard_map/reshape | solution.py:330
  508.4 3.9 pad_maximum_fusion
  512.6 5.5 convolution_convert_fusion.4
  518.0 6.0 reshape.807
  534.0 4.9 convolution_convert_fusion.2
  538.8 9.8 %reshape.810 = bf16[16,48,4,768]{3,2,1,0:T(4,128)(2,1)} reshape(bf16[768,3072]{1,0:T(8,128)(2,1)} %convolution_convert_fusion.2) | data formatting | bytes 9437184 | tf_op jit(solution)/shard_map/reshape | solution.py:330
  561.1 6.3 add_convert_fusion
  575.9 4.7 collective-permute-done.4
  580.8 93.5 %reduce-scatter.8.cloned.1.call-done = bf16[1,384,768]{2,1,0:T(8,128)(2,1)} async-done(((bf16[16,384,768]{2,1,0:T(8,128)(2,1)}), bf16[1,384,768]{2,1,0:T(8,128)(2,1)}) %reduce-scatter.8.cloned.1.call-update) | async-done | bytes 589840 | tf_op jit(solution)/shard_map/reduce_scatter | solution.py:395
  678.4 145.5 %reduce-scatter.6.cloned.1.call-done = bf16[1,576,768]{2,1,0:T(8,128)(2,1)} async-done(((bf16[16,576,768]{2,1,0:T(8,128)(2,1)}), bf16[1,576,768]{2,1,0:T(8,128)(2,1)}) %reduce-scatter.6.cloned.1.call-update) | async-done | bytes 884752 | tf_op jit(solution)/shard_map/reduce_scatter | solution.py:395
  827.1 17.6 %collective-permute-done.5 = bf16[576,768]{1,0:T(8,128)(2,1)} collective-permute-done((bf16[576,768]{1,0:T(8,128)(2,1)}, bf16[576,768]{1,0:T(8,128)(2,1)}, u32[]{:S(2)}, u32[]{:S(2)}) %collective-permute-start.5) | collective-permute-done | bytes 884768 | tf_op jit(solution)/shard_map/ppermute | solution.py:204
  (564 shorter events, 194.8 us)
Async XLA Ops:
  7.2 8.6 copy-start.61
  7.2 59.4 %all-gather.7.cloned.1.call-start = ((), (), s32[]{:S(2)}) async-start(), calls=%async_computation.6 | async-start | bytes 3969024 | tf_op jit(solution)/shard_map/all_gather | solution.py:256
  15.7 140.8 %all-gather.11.cloned.1.call-start = ((), (), s32[]{:S(2)}) async-start(), calls=%async_computation.8 | async-start | bytes 11280384 | tf_op jit(solution)/shard_map/all_gather | solution.py:256
  17.2 250.6 %all-gather.9.cloned.1.call-start = ((), (), s32[]{:S(2)}) async-start(), calls=%async_computation.7 | async-start | bytes 15040512 | tf_op jit(solution)/shard_map/all_gather | solution.py:256
  19.1 552.3 %reduce-scatter.4.cloned.1.call-start = ((), (), s32[]{:S(2)}) async-start(), calls=%async_computation.3 | async-start | bytes 5431296 | tf_op jit(solution)/shard_map/reduce_scatter | solution.py:395
  24.2 46.0 %copy-start.90 = (f32[512]{0:T(512)}, f32[512]{0:T(512)S(1)}, u32[]{:S(2)}) copy-start(f32[512]{0:T(512)S(1)} %fusion.87) | copy-start | bytes 6148
  68.8 209.1 %copy-start.117 = (f32[3072]{0:T(1024)}, f32[3072]{0:T(1024)S(1)}, u32[]{:S(2)}) copy-start(f32[3072]{0:T(1024)S(1)} %add.293) | copy-start | bytes 36868
  69.5 208.5 %copy-start.112 = (f32[768]{0:T(1024)}, f32[768]{0:T(1024)S(1)}, u32[]{:S(2)}) copy-start(f32[768]{0:T(1024)S(1)} %get-tuple-element.55) | copy-start | bytes 9220
  69.5 208.5 %copy-start.130 = (f32[768]{0:T(1024)}, f32[768]{0:T(1024)S(1)}, u32[]{:S(2)}) copy-start(f32[768]{0:T(1024)S(1)} %get-tuple-element.54) | copy-start | bytes 9220
  70.5 11.3 %collective-permute-start = (bf16[256,768]{1,0:T(8,128)(2,1)S(1)}, bf16[256,768]{1,0:T(8,128)(2,1)S(1)}, u32[]{:S(2)}, u32[]{:S(2)}) collective-permute-start(bf16[256,768]{1,0:T(8,128)(2,1)S(1)} %slice.510), channel_id=1, source_target_pairs={{0,16},{16,0},{1,17},{17,1},{2,18},{18,2},{3,19},{19,3},{4,20},{20... | collective-permute-start | bytes 1179656 | tf_op jit(solution)/shard_map/ppermute | solution.py:204
  270.5 13.8 %copy-start.15 = (bf16[16,192,768]{2,1,0:T(8,128)(2,1)}, bf16[16,192,768]{2,1,0:T(8,128)(2,1)S(1)}, u32[]{:S(2)}) copy-start(bf16[16,192,768]{2,1,0:T(8,128)(2,1)S(1)} %slice.523) | copy-start | bytes 14155780
  276.5 7.8 copy-start.46
  276.5 13.3 %copy-start.14 = (bf16[16,48,768]{2,1,0:T(8,128)(2,1)}, bf16[16,48,768]{2,1,0:T(8,128)(2,1)S(1)}, u32[]{:S(2)}) copy-start(bf16[16,48,768]{2,1,0:T(8,128)(2,1)S(1)} %get-tuple-element.77) | copy-start | bytes 3538948
  276.5 23.1 %copy-start.49 = (bf16[16,48,768]{2,1,0:T(8,128)(2,1)}, bf16[16,48,768]{2,1,0:T(8,128)(2,1)S(1)}, u32[]{:S(2)}) copy-start(bf16[16,48,768]{2,1,0:T(8,128)(2,1)S(1)} %get-tuple-element.75) | copy-start | bytes 3538948
  276.5 23.1 %copy-start.51 = (bf16[16,48,768]{2,1,0:T(8,128)(2,1)}, bf16[16,48,768]{2,1,0:T(8,128)(2,1)S(1)}, u32[]{:S(2)}) copy-start(bf16[16,48,768]{2,1,0:T(8,128)(2,1)S(1)} %get-tuple-element.76) | copy-start | bytes 3538948
  288.3 11.3 %collective-permute-start.1 = (bf16[256,768]{1,0:T(8,128)(2,1)S(1)}, bf16[256,768]{1,0:T(8,128)(2,1)S(1)}, u32[]{:S(2)}, u32[]{:S(2)}) collective-permute-start(bf16[256,768]{1,0:T(8,128)(2,1)S(1)} %slice.532), channel_id=1, source_target_pairs={{0,16},{16,0},{1,17},{17,1},{2,18},{18,2},{3,19},{19,3},{4,20},{20... | collective-permute-start | bytes 1179656 | tf_op jit(solution)/shard_map/ppermute | solution.py:204
  315.4 10.7 %slice-start = ((s8[4718592]{0:T(1024)(128)(4,1)}), s8[4194304]{0:T(1024)(128)(4,1)S(1)}, s32[]{:S(2)}) async-start(s8[4718592]{0:T(1024)(128)(4,1)} %bitcast.239), calls=%async_computation.9 | async-start | bytes 8388608
  317.9 19.9 %copy-start.13 = (f32[512,768]{1,0:T(8,128)}, f32[512,768]{1,0:T(8,128)S(1)}, u32[]{:S(2)}) copy-start(f32[512,768]{1,0:T(8,128)S(1)} %get-tuple-element.158) | copy-start | bytes 4718596
  318.0 19.8 %copy-start.97 = (f32[512]{0:T(512)}, f32[512]{0:T(512)S(1)}, u32[]{:S(2)}) copy-start(f32[512]{0:T(512)S(1)} %broadcast_multiply_fusion) | copy-start | bytes 6148
  318.3 19.5 %copy-start.126 = (f32[512]{0:T(512)}, f32[512]{0:T(512)S(1)}, u32[]{:S(2)}) copy-start(f32[512]{0:T(512)S(1)} %fusion.90) | copy-start | bytes 6148
  326.2 7.0 copy-start.56
  326.2 7.0 copy-start.57
  339.7 53.8 %copy-start.7 = (bf16[512,768]{1,0:T(8,128)(2,1)}, bf16[512,768]{1,0:T(8,128)(2,1)S(1)}, u32[]{:S(2)}) copy-start(bf16[512,768]{1,0:T(8,128)(2,1)S(1)} %get-tuple-element.70) | copy-start | bytes 2359300
  371.1 19.7 %collective-permute-start.2 = (bf16[256,768]{1,0:T(8,128)(2,1)}, bf16[256,768]{1,0:T(8,128)(2,1)S(1)}, u32[]{:S(2)}, u32[]{:S(2)}) collective-permute-start(bf16[256,768]{1,0:T(8,128)(2,1)} %convolution_convert_fusion.12), channel_id=1, source_target_pairs={{0,16},{16,0},{1,17},{17,1},{2,18},{18,2},{3,19},{19,3},{4,20},{20... | collective-permute-start | bytes 1179656 | tf_op jit(solution)/shard_map/ppermute | solution.py:204
  411.7 20.4 %copy-start.30 = (bf16[512,768]{1,0:T(8,128)(2,1)S(1)}, bf16[512,768]{1,0:T(8,128)(2,1)}, u32[]{:S(2)}) copy-start(bf16[512,768]{1,0:T(8,128)(2,1)} %copy-done.29) | copy-start | bytes 2359300
  440.3 34.0 %collective-permute-start.3 = (bf16[256,768]{1,0:T(8,128)(2,1)}, bf16[256,768]{1,0:T(8,128)(2,1)S(1)}, u32[]{:S(2)}, u32[]{:S(2)}) collective-permute-start(bf16[256,768]{1,0:T(8,128)(2,1)} %fusion.34), channel_id=1, source_target_pairs={{0,16},{16,0},{1,17},{17,1},{2,18},{18,2},{3,19},{19,3},{4,20},{20... | collective-permute-start | bytes 1179656 | tf_op jit(solution)/shard_map/ppermute | solution.py:204
  483.8 190.4 %reduce-scatter.8.cloned.1.call-start = ((), (), s32[]{:S(2)}) async-start(), calls=%async_computation.5 | async-start | bytes 10027008 | tf_op jit(solution)/shard_map/reduce_scatter | solution.py:395
  512.3 311.6 %reduce-scatter.6.cloned.1.call-start = ((), (), s32[]{:S(2)}) async-start(), calls=%async_computation.4 | async-start | bytes 15040512 | tf_op jit(solution)/shard_map/reduce_scatter | solution.py:395
  571.4 9.2 %collective-permute-start.4 = (bf16[208,768]{1,0:T(8,128)(2,1)}, bf16[208,768]{1,0:T(8,128)(2,1)S(1)}, u32[]{:S(2)}, u32[]{:S(2)}) collective-permute-start(bf16[208,768]{1,0:T(8,128)(2,1)} %bitcast.298), channel_id=1, source_target_pairs={{0,16},{16,0},{1,17},{17,1},{2,18},{18,2},{3,19},{19,3},{4,20},{20... | collective-permute-start | bytes 958472 | tf_op jit(solution)/shard_map/ppermute | solution.py:204
  674.3 151.9 %collective-permute-start.6 = (bf16[384,768]{1,0:T(8,128)(2,1)}, bf16[384,768]{1,0:T(8,128)(2,1)S(1)}, u32[]{:S(2)}, u32[]{:S(2)}) collective-permute-start(bf16[384,768]{1,0:T(8,128)(2,1)} %bitcast.297), channel_id=1, source_target_pairs={{0,16},{16,0},{1,17},{17,1},{2,18},{18,2},{3,19},{19,3},{4,20},{20... | collective-permute-start | bytes 1769480 | tf_op jit(solution)/shard_map/ppermute | solution.py:204
  677.6 148.6 %copy-start.64 = (bf16[1,384,768]{2,1,0:T(8,128)(2,1)S(1)}, bf16[1,384,768]{2,1,0:T(8,128)(2,1)}, u32[]{:S(2)}) copy-start(bf16[1,384,768]{2,1,0:T(8,128)(2,1)} %reduce-scatter.8.cloned.1.call-done) | copy-start | bytes 1769476
  824.0 20.8 %collective-permute-start.5 = (bf16[576,768]{1,0:T(8,128)(2,1)}, bf16[576,768]{1,0:T(8,128)(2,1)}, u32[]{:S(2)}, u32[]{:S(2)}) collective-permute-start(bf16[576,768]{1,0:T(8,128)(2,1)} %bitcast.293), channel_id=1, source_target_pairs={{0,16},{16,0},{1,17},{17,1},{2,18},{18,2},{3,19},{19,3},{4,20},{20... | collective-permute-start | bytes 2654216 | tf_op jit(solution)/shard_map/ppermute | solution.py:204
  (134 other events, 332.1 us)
Sparse Core Ops, SparseCore 0:
  15.8 50.6 all-gather.6
  69.4 87.0 all-gather.10
  159.4 108.3 all-gather.8
  484.0 75.8 reduce-scatter.3
  563.8 110.3 reduce-scatter.7
  678.3 145.6 reduce-scatter.5

commit v2 on v1

--- a/solution.py
+++ b/solution.py
@@ -117,7 +117,7 @@
 
 
 def attend_back_kernel(
-    seg_row, seg_col, valid_col, q_ref, kv_ref, halo_ref, grad_ref, lse_ref, dq_ref, dkv_ref, dhalo_ref, bias
+    seg_row, seg_col, valid_col, q_ref, kv_ref, halo_ref, grad_ref, lse_ref, _, dq_ref, dkv_ref, dhalo_ref, bias
 ):
     @pl.when(pl.program_id(0) == 0)
     def _():
@@ -169,7 +169,7 @@
     dhalo_ref[:, PAIR:] = dv_halo.astype(BF16)
 
 
-def attend_back(segment, valid, queries, pairs, halo_pairs, grads, lse):
+def attend_back(segment, valid, queries, pairs, halo_pairs, grads, lse, earlier):
     rows, reach = queries.shape[0], segment.shape[0]
     whole = lambda shape: pl.BlockSpec(shape, lambda i: (0, 0))
     tokens = pl.BlockSpec((rows, PAIR), lambda i: (0, i))
@@ -187,6 +187,7 @@
             halo,
             tokens,
             pl.BlockSpec((1, 2, rows), lambda i: (i, 0, 0)),
+            pl.BlockSpec(memory_space=pl.ANY),
         ],
         out_specs=[tokens, both, halo],
         out_shape=[
@@ -197,7 +198,7 @@
         scratch_shapes=[pltpu.VMEM((reach, rows), F32)],
         cost_estimate=pl.CostEstimate(flops=10 * 5 * 65536 * D, bytes_accessed=10 << 20, transcendentals=5 * 65536 * 12),
         name="attend_back",
-    )(segment[None, :rows], segment[:, None], valid[:, None], queries, pairs, halo_pairs, grads, lse)
+    )(segment[None, :rows], segment[:, None], valid[:, None], queries, pairs, halo_pairs, grads, lse, earlier)
 
 
 def swap_seq(values):
@@ -212,9 +213,206 @@
     return matrix.reshape(-1, PAIRS, 2, PAIR).swapaxes(1, 2).reshape(-1, 2 * D)
 
 
-def column_blocks(matrix):
-    rows = matrix.shape[0]
-    return matrix.reshape(rows, -1, D).swapaxes(0, 1).reshape(-1, D)
+HOPS = 16
+
+
+def place(z, y, core):
+    return (z * 2 + y) * 2 + core
+
+
+def hop(values, target):
+    pairs = []
+    for z in range(4):
+        for y in range(2):
+            for core in range(2):
+                goal = target(z, y, core)
+                if goal is not None:
+                    pairs.append((place(z, y, core), place(*goal)))
+    return lax.ppermute(values, "fsdp", pairs)
+
+
+def hop_core(values):
+    return hop(values, lambda z, y, core: (z, y, 1 - core))
+
+
+def hop_y(values):
+    return hop(values, lambda z, y, core: (z, 1 - y, core))
+
+
+def hop_z(values, table):
+    return hop(values, lambda z, y, core: None if z not in table else (table[z], y, core))
+
+
+def up(values, sources=(0, 1, 2)):
+    return hop(values, lambda z, y, core: (z + 1, y, core) if z in sources else None)
+
+
+def down(values, sources=(1, 2, 3)):
+    return hop(values, lambda z, y, core: (z - 1, y, core) if z in sources else None)
+
+
+def pick(values, index, axis):
+    return lax.dynamic_index_in_dim(values, index, axis, keepdims=False)
+
+
+def half_of(values, x):
+    half = values.shape[-1] // 2
+    return lax.dynamic_slice_in_dim(values, x * half, half, axis=values.ndim - 1)
+
+
+def side_by_side(blocks):
+    rows = D // HOPS
+    count = blocks.shape[-2] // rows
+    return jnp.concatenate([blocks[..., j * rows : (j + 1) * rows, :] for j in range(count)], axis=-1)
+
+
+def gather_hops(rise_shard, fall_shard, name):
+    x = lax.axis_index("seq")
+    with jax.named_scope(name):
+        mine = jnp.concatenate([half_of(rise_shard, x), side_by_side(half_of(fall_shard, x))], axis=1)
+        with jax.named_scope("up1"):
+            up_one = up(mine)
+        with jax.named_scope("down1"):
+            down_one = down(mine)
+        with jax.named_scope("up2"):
+            up_two = up(up_one, (1, 2))
+        with jax.named_scope("down2"):
+            down_two = down(down_one, (1, 2))
+        with jax.named_scope("up3"):
+            up_three = up(up_two, (2,))
+        with jax.named_scope("down3"):
+            down_three = down(down_two, (1,))
+        line = jnp.stack([mine, down_one + up_three, down_two + up_two, down_three + up_one])
+        split = mine.shape[1] // 2
+        line_a, line_b = line[:, :, :split], line[:, :, split:]
+        with jax.named_scope("y1"):
+            first_a = jnp.concatenate([line_a, hop_y(line_a)], axis=0)
+        with jax.named_scope("x1"):
+            first_b = jnp.concatenate([line_b, swap_seq(line_b)], axis=0)
+        with jax.named_scope("x2"):
+            second_a = swap_seq(first_a)
+        with jax.named_scope("y2"):
+            second_b = hop_y(first_b)
+        with jax.named_scope("c1"):
+            third_a = hop_core(first_a)
+        with jax.named_scope("c2"):
+            third_b = hop_core(first_b)
+        with jax.named_scope("c3"):
+            fourth_a = hop_core(second_a)
+        with jax.named_scope("c4"):
+            fourth_b = hop_core(second_b)
+    return [first_a, second_a, third_a, fourth_a, first_b, second_b, third_b, fourth_b]
+
+
+def along_z(line, name):
+    z = lax.axis_index("fsdp") // 4
+    rising = falling = None
+    with jax.named_scope(name):
+        for step in (3, 2, 1):
+            low, high = pick(line, jnp.minimum(z + step, 3), 0), pick(line, jnp.maximum(z - step, 0), 0)
+            with jax.named_scope(f"up{step}"):
+                rising = up(low if rising is None else low + rising, tuple(range(4 - step)))
+            with jax.named_scope(f"down{step}"):
+                falling = down(high if falling is None else high + falling, tuple(range(step, 4)))
+        return (pick(line, z, 0).astype(F32) + rising.astype(F32) + falling.astype(F32)).astype(BF16)
+
+
+def reduce_core(matrix):
+    core = lax.axis_index("fsdp") % 2
+    both = matrix.reshape(8, 2, -1, matrix.shape[-1])
+    return [pick(both, core, 1), hop_core(pick(both, 1 - core, 1))]
+
+
+def total(terms):
+    result = terms[0].astype(F32)
+    for term in terms[1:]:
+        result = result + term.astype(F32)
+    return result.astype(BF16)
+
+
+def sent_x(terms):
+    x = lax.axis_index("seq")
+    return [half_of(term, x) for term in terms] + [swap_seq(total([half_of(term, 1 - x) for term in terms]))]
+
+
+def sent_y(terms):
+    y = (lax.axis_index("fsdp") // 2) % 2
+    terms = [term.reshape((4, 2) + term.shape[1:]) for term in terms]
+    return [pick(term, y, 1) for term in terms] + [hop_y(total([pick(term, 1 - y, 1) for term in terms]))]
+
+
+def reduce_line(first_x, first_y, name):
+    with jax.named_scope(name):
+        with jax.named_scope("x1"):
+            first_x = sent_x(first_x)
+        with jax.named_scope("y1"):
+            first_y = sent_y(first_y)
+        with jax.named_scope("y2"):
+            first_x = total(sent_y(first_x))
+        with jax.named_scope("x2"):
+            first_y = total(sent_x(first_y))
+    return first_x, first_y
+
+
+def both_halves(mine, other, start, size):
+    here, there = mine[:, start : start + size], other[:, start : start + size]
+    left = lax.axis_index("seq") == 0
+    return jnp.concatenate([jnp.where(left, here, there), jnp.where(left, there, here)], axis=1).astype(F32)
+
+
+def assemble_kernel(*refs):
+    sources, (rise, fall, held_rise, held_fall, in_sems, out_sems) = refs[:8], refs[-6:]
+    my_x, me = lax.axis_index("seq"), lax.axis_index("fsdp")
+    my_core, my_y, my_z = me % 2, (me // 2) % 2, me // 4
+    z_of = [(my_z + slot) % 4 for slot in range(4)]
+    rows = D // HOPS
+    for index, source in enumerate(sources):
+        is_rise, other_core, second = index < 4, (index % 4) // 2, index % 2
+        core = (my_core + other_core) % 2
+        for slot in range(8):
+            turn, z = slot // 4, z_of[slot % 4]
+            x = (my_x + (second if is_rise else turn)) % 2
+            y = (my_y + (turn if is_rise else second)) % 2
+            owner = (z * 2 + y) * 2 + core
+            if is_rise:
+                pltpu.make_async_copy(
+                    source.at[slot],
+                    held_rise.at[
+                        pl.ds(pl.multiple_of(owner * rows, 16), rows),
+                        pl.ds(pl.multiple_of(x * (FF // 2), 128), FF // 2),
+                    ],
+                    in_sems.at[0],
+                ).start()
+                continue
+            for block in range(4):
+                pltpu.make_async_copy(
+                    source.at[slot, :, pl.ds(block * (D // 2), D // 2)],
+                    held_fall.at[
+                        pl.ds(pl.multiple_of((owner * 4 + block) * rows, 16), rows),
+                        pl.ds(pl.multiple_of(x * (D // 2), 128), D // 2),
+                    ],
+                    in_sems.at[1],
+                ).start()
+    for which, (held, out) in enumerate(((held_rise, rise), (held_fall, fall))):
+        pltpu.make_async_copy(held, held, in_sems.at[which]).wait()
+        pltpu.make_async_copy(held, out, out_sems.at[which]).start()
+    for which, (held, out) in enumerate(((held_rise, rise), (held_fall, fall))):
+        pltpu.make_async_copy(held, out, out_sems.at[which]).wait()
+
+
+def assemble(buffers, earlier):
+    shapes = [(D, FF), (FF, D)]
+    return pl.pallas_call(
+        assemble_kernel,
+        in_specs=[pl.BlockSpec(memory_space=pl.ANY)] * 9,
+        out_specs=[pl.BlockSpec(memory_space=pl.ANY)] * 2,
+        out_shape=[jax.ShapeDtypeStruct(shape, BF16) for shape in shapes],
+        scratch_shapes=[pltpu.VMEM(shape, BF16) for shape in shapes]
+        + [pltpu.SemaphoreType.DMA((2,)), pltpu.SemaphoreType.DMA((2,))],
+        compiler_params=pltpu.CompilerParams(vmem_limit_bytes=24 << 20),
+        cost_estimate=pl.CostEstimate(flops=0, bytes_accessed=4 * 2 * D * FF, transcendentals=0),
+        name="assemble",
+    )(*buffers, earlier)
 
 
 def local(
@@ -257,53 +455,43 @@
 
     segment, valid = by_block(segment_ids[0]), by_block(key_valid[0])
 
-    ordered = [
-        jnp.concatenate([input_weight[depth][:, :D], pair_columns(input_weight[depth][:, D:])], axis=1)
-        for depth in range(LAYERS)
-    ]
     smalls = [first_gain, first_shift, query_bias, value_bias, output_bias, second_gain, second_shift, down_bias]
     small = jnp.concatenate(
         [member.reshape(LAYERS, 1, rows_of) for member in smalls] + [up_bias.reshape(LAYERS, 4, rows_of)], axis=1
     ).reshape(-1)
     side = rows_of * 128
     small_block = jnp.pad(small, (0, side - small.shape[0])).reshape(rows_of, 128)
-    first = gather(jnp.concatenate([ordered[0], small_block], axis=1))
-
-    def rest(depth):
-        return [output_weight[depth], column_blocks(up_weight[depth]), down_weight[depth]]
-
-    second = gather(jnp.concatenate(rest(0) + [column_blocks(ordered[1])], axis=0))
-    third = gather(jnp.concatenate(rest(1), axis=0))
-
-    def take(packed, start, count):
-        part = packed[:, start * rows_of : (start + count) * rows_of]
-        return part
-
-    def joined(packed, start, count):
-        return jnp.concatenate(
-            [take(packed, start + j, 1).reshape(D, D) for j in range(count)], axis=1
-        )
-
-    def unpacked(packed):
-        return take(packed, 0, 1).reshape(D, D), joined(packed, 1, 4), take(packed, 5, 4).reshape(FF, D)
-
-    first = first.reshape(D, -1)
-    mix_weights = [first[:, : 3 * D], joined(second, 9, 3)]
-    mlp_weights = [unpacked(second), unpacked(third)]
+
+    def mixing(depth):
+        return [input_weight[depth][:, :D], pair_columns(input_weight[depth][:, D:]), output_weight[depth]]
+
+    with jax.named_scope("mixing0"):
+        low = gather(jnp.concatenate(mixing(0) + [small_block], axis=1)).reshape(D, -1)
+    with jax.named_scope("mixing1"):
+        high = gather(jnp.concatenate(mixing(1), axis=1)).reshape(D, -1)
+    mix_weights = [low[:, : 3 * D], high[:, : 3 * D]]
+    out_weights = [low[:, 3 * D : 4 * D], high[:, 3 * D : 4 * D]]
     smalls_full = (
-        first[:, 3 * D :].reshape(owners, side)[:, : small.shape[0]].reshape(owners, LAYERS, 12, rows_of).astype(F32)
+        low[:, 4 * D :].reshape(owners, side)[:, : small.shape[0]].reshape(owners, LAYERS, 12, rows_of).astype(F32)
     )
     vectors = smalls_full[:, :, :8].transpose(1, 2, 0, 3).reshape(LAYERS, 8, D)
     up_biases = smalls_full[:, :, 8:].transpose(1, 0, 2, 3).reshape(LAYERS, FF)
+    by_hops = owners == HOPS
+    if by_hops:
+        pieces = [gather_hops(up_weight[depth], down_weight[depth], f"gather{depth}") for depth in range(LAYERS)]
+
+    def feed_weights(depth, earlier):
+        if by_hops:
+            return assemble(pieces[depth], earlier)
+        return gather(up_weight[depth]).reshape(D, FF), gather(down_weight[depth]).reshape(FF, D)
 
     stream = near_first(layer_input[0]).astype(F32)
-    kept = []
+    kept, feed = [], []
     for depth in range(LAYERS):
         gain_one, shift_one, query_shift, value_shift, out_shift, gain_two, shift_two, fall_shift = [
             vectors[depth, j] for j in range(8)
         ]
-        mix_weight = mix_weights[depth]
-        out_weight, rise_weight, fall_weight = mlp_weights[depth]
+        mix_weight, out_weight = mix_weights[depth], out_weights[depth]
         normed = layer_norm(stream, gain_one, shift_one).astype(BF16)
         halo_normed = swap_seq(normed[:HALF])
         pair_shift = jnp.stack([jnp.zeros((PAIRS, PAIR), F32), value_shift.reshape(PAIRS, PAIR)], axis=1).reshape(-1)
@@ -313,6 +501,8 @@
         attended, lse = attend(segment, valid, queries, pairs, halo_pairs)
         stream_mid = stream + (dot(attended, out_weight) + out_shift)
         normed_two = layer_norm(stream_mid, gain_two, shift_two).astype(BF16)
+        rise_weight, fall_weight = feed_weights(depth, attended)
+        feed.append((rise_weight, fall_weight))
         before = dot(normed_two, rise_weight) + up_biases[depth]
         hidden = gelu_exact(before).astype(BF16)
         stream_next = stream_mid + (dot(hidden, fall_weight) + fall_shift)
@@ -320,43 +510,61 @@
         stream = stream_next
 
     grad_stream = near_first(output_cotangent[0]).astype(F32)
-    packs = {}
     small_grads = [None] * LAYERS
 
-    def owned_rows(matrix):
-        return matrix.astype(BF16).reshape(owners, -1, D)
-
-    def owned_blocks(matrix):
-        blocks = matrix.astype(BF16).reshape(owners, rows_of, -1, D)
-        return blocks.swapaxes(1, 2).reshape(owners, -1, D)
+    def scattered(matrix):
+        return lax.psum_scatter(matrix, "fsdp", scatter_dimension=0, tiled=True)
+
+    def over_seq(mine):
+        return mine.astype(F32) + swap_seq(mine).astype(F32)
+
+    def blocks_of(matrix):
+        return [matrix[:, at : at + D].reshape(owners, rows_of, D) for at in range(0, matrix.shape[1], D)]
 
     for depth in reversed(range(LAYERS)):
         gain_one, shift_one, query_shift, value_shift, out_shift, gain_two, shift_two, fall_shift = [
             vectors[depth, j] for j in range(8)
         ]
-        mix_weight = mix_weights[depth]
-        out_weight, rise_weight, fall_weight = mlp_weights[depth]
+        mix_weight, out_weight = mix_weights[depth], out_weights[depth]
+        rise_weight, fall_weight = feed[depth]
         (stream_in, normed, halo_normed, queries, pairs, halo_pairs, lse, attended, stream_mid, normed_two, before, hidden) = kept[depth]
         grad_fall = grad_stream.astype(BF16)
-        fall_weight_grad = dot_rows(hidden, grad_fall)
+        fall_grad = dot_rows(hidden, grad_fall).astype(BF16)
         fall_shift_grad = column_sum(grad_fall)
         grad_before = (dot_back(grad_fall, fall_weight) * gelu_slope(before)).astype(BF16)
-        rise_weight_grad = dot_rows(normed_two, grad_before)
+        rise_grad = dot_rows(normed_two, grad_before).astype(BF16)
         rise_shift_grad = column_sum(grad_before)
         grad_normed_two = dot_back(grad_before, rise_weight)
         norm_pair_two = jax.vjp(layer_norm, stream_mid, gain_two, shift_two)
         grad_mid_norm, gain_two_grad, shift_two_grad = norm_pair_two[1](grad_normed_two)
         grad_mid = grad_stream + grad_mid_norm
         grad_branch = grad_mid.astype(BF16)
-        out_weight_grad = dot_rows(attended, grad_branch)
+        out_grad = dot_rows(attended, grad_branch).astype(BF16)
         out_shift_grad = column_sum(grad_branch)
         grad_attended = dot_back(grad_branch, out_weight).astype(BF16)
-        dq, dpairs, dhalo = attend_back(segment, valid, queries, pairs, halo_pairs, grad_attended, lse)
+        if depth == 0 and by_hops:
+            with jax.named_scope("feed_core"):
+                feed_terms = reduce_core(rise_grad), reduce_core(fall_grad)
+            feed_line = reduce_line(*feed_terms, "feed")
+        with jax.named_scope(f"back{depth}"):
+            dq, dpairs, dhalo = attend_back(segment, valid, queries, pairs, halo_pairs, grad_attended, lse, rise_grad)
         halo_back = swap_seq(dot_back(dhalo, mix_weight[:, D:]).astype(BF16)).astype(F32)
         normed_all = jnp.concatenate([normed, halo_normed], axis=0)
         dpairs_all = jnp.concatenate([dpairs, dhalo], axis=0)
-        query_weight_grad = dot_rows(normed, dq)
-        pair_weight_grad = dot_rows(normed_all, dpairs_all)
+        query_grad = dot_rows(normed, dq).astype(BF16)
+        pair_grad = dot_rows(normed_all, dpairs_all).astype(BF16)
+        if depth == 1:
+            parts = [fall_grad.reshape(owners, -1, D)]
+            for matrix in (rise_grad, out_grad, query_grad, pair_grad):
+                parts += blocks_of(matrix)
+            with jax.named_scope("scatter1"):
+                high_sum = scattered(jnp.concatenate(parts, axis=1).reshape(-1, D))
+        elif by_hops:
+            with jax.named_scope("mix_core"):
+                mix_terms = [reduce_core(matrix) for matrix in (pair_grad, query_grad, out_grad)]
+            pair_terms = mix_terms[0]
+            rest_terms = [jnp.concatenate([a, b], axis=-1) for a, b in zip(mix_terms[1], mix_terms[2])]
+            mix_line = reduce_line(pair_terms, rest_terms, "mix")
         query_shift_grad = column_sum(dq)
         value_shift_grad = column_sum(dpairs_all).reshape(PAIRS, 2, PAIR)[:, 1].reshape(D)
         grad_normed = dot_back(dq, mix_weight[:, :D]) + dot_back(dpairs, mix_weight[:, D:])
@@ -364,11 +572,6 @@
         norm_pair_one = jax.vjp(layer_norm, stream_in, gain_one, shift_one)
         grad_in_norm, gain_one_grad, shift_one_grad = norm_pair_one[1](grad_normed)
         grad_stream = grad_mid + grad_in_norm
-        packs["fall", depth] = owned_rows(fall_weight_grad)
-        packs["rise", depth] = owned_blocks(rise_weight_grad)
-        packs["out", depth] = owned_rows(out_weight_grad)
-        packs["query", depth] = owned_rows(query_weight_grad)
-        packs["pair", depth] = owned_blocks(pair_weight_grad)
         small_grads[depth] = jnp.concatenate(
             [
                 member.reshape(owners, 1, rows_of)
@@ -387,36 +590,50 @@
             axis=1,
         )
 
-    small_all = jnp.concatenate(small_grads, axis=1).astype(BF16).reshape(owners, -1)
-    small_all = jnp.pad(small_all, ((0, 0), (0, 16 * D - small_all.shape[1]))).reshape(owners, 16, D)
-
-    def reduced(names):
-        parts = [packs[name] for name in names]
-        mine = lax.psum_scatter(jnp.concatenate(parts, axis=1), "fsdp", scatter_dimension=0, tiled=False)
-        total = mine.astype(F32) + swap_seq(mine).astype(F32)
-        found, at = {}, 0
-        for name, part in zip(names, parts):
-            found[name] = total[at : at + part.shape[1]]
-            at += part.shape[1]
-        return found
-
-    packs["small", 0] = small_all
-    sums = reduced([("fall", 1), ("rise", 1)])
-    sums.update(reduced([("out", 1), ("query", 1), ("pair", 1), ("fall", 0), ("rise", 0)]))
-    sums.update(reduced([("out", 0), ("query", 0), ("pair", 0), ("small", 0)]))
+    small_all = jnp.concatenate(small_grads, axis=1).reshape(owners, -1)
+    high_sum = over_seq(high_sum)
 
     def columns(block_rows, count):
         return block_rows.reshape(count, rows_of, D).swapaxes(0, 1).reshape(rows_of, count * D)
 
-    def both(fn):
-        return jnp.stack([fn(depth) for depth in range(LAYERS)])
-
-    small_sum = sums["small", 0].reshape(-1)[: small.shape[0]].reshape(LAYERS, 12, rows_of)
-    mix_out = both(
-        lambda depth: jnp.concatenate(
-            [sums["query", depth], unpair_columns(columns(sums["pair", depth], 2))], axis=1
+    at = [0, 4, 8, 9, 10, 12]
+    fall_high, rise_high, out_high, query_high, pair_high = [
+        high_sum[rows_of * low_row : rows_of * high_row] for low_row, high_row in zip(at[:-1], at[1:])
+    ]
+    rise_high, pair_high = columns(rise_high, 4), columns(pair_high, 2)
+    if by_hops:
+        rise_line, fall_line = feed_line
+        mine = along_z(jnp.concatenate([rise_line, side_by_side(fall_line)], axis=-1), "feed")
+        with jax.named_scope("feed_last"):
+            other = swap_seq(mine)
+        rise_low = both_halves(mine, other, 0, FF // 2)
+        fall_low = jnp.concatenate(
+            [both_halves(mine, other, FF // 2 + j * D // 2, D // 2) for j in range(4)], axis=0
         )
-    )
+        with jax.named_scope("small"):
+            small_all = small_all + hop_core(small_all)
+            small_all = small_all + hop_y(small_all)
+            small_all = small_all + swap_seq(small_all)
+        me = lax.axis_index("fsdp")
+        small_line = pick(small_all.reshape(4, 4, -1), me % 4, 1).astype(BF16).reshape(4, rows_of, -1)
+        width = small_line.shape[-1]
+        small_line = jnp.pad(small_line, ((0, 0), (0, 0), (0, 128 - width)))
+        mine = along_z(jnp.concatenate([*mix_line, small_line], axis=-1), "mix")
+        with jax.named_scope("mix_last"):
+            other = swap_seq(mine[:, : 2 * D])
+        pair_low = both_halves(mine, other, 0, D)
+        rest_low = both_halves(mine, other, D, D)
+        query_low, out_low = rest_low[:, :D], rest_low[:, D:]
+        small_sum = mine[:, 2 * D : 2 * D + width].astype(F32).reshape(LAYERS, 12, rows_of)
+    else:
+        fall_low, rise_low, out_low, query_low, pair_low = [
+            over_seq(scattered(matrix)) for matrix in (fall_grad, rise_grad, out_grad, query_grad, pair_grad)
+        ]
+        small_sum = over_seq(scattered(small_all.astype(BF16))).reshape(LAYERS, 12, rows_of)
+
+    def mix_out(query, pair):
+        return jnp.concatenate([query, unpair_columns(pair)], axis=1)
+
     layer_output = near_first(stream.astype(BF16))[None]
     input_grad = near_first(grad_stream)[None]
     return (
@@ -424,16 +641,16 @@
         input_grad,
         small_sum[:, 0],
         small_sum[:, 1],
-        mix_out,
+        jnp.stack([mix_out(query_low, pair_low), mix_out(query_high, pair_high)]),
         small_sum[:, 2],
         small_sum[:, 3],
-        both(lambda depth: sums["out", depth]),
+        jnp.stack([out_low, out_high]),
         small_sum[:, 4],
         small_sum[:, 5],
         small_sum[:, 6],
-        both(lambda depth: columns(sums["rise", depth], 4)),
+        jnp.stack([rise_low, rise_high]),
         small_sum[:, 8:].reshape(LAYERS, 4 * rows_of),
-        both(lambda depth: sums["fall", depth]),
+        jnp.stack([fall_low, fall_high]),
         small_sum[:, 7],
     )
 

time: 869 us -> 609 us (0.70)
  waiting for transfers between devices: 472 us -> 169 us
  starting transfers between devices: 10 us -> 78.3 us
  local copies, waits for them, and re-layouts: 147 us -> 91.9 us
  other arithmetic: 33.4 us -> 51.8 us
    reduce_scatter x3 -> x1, waiting for transfers between devices: 239 us -> 0.02 us  [scattered(): return lax.psum_scatter(matrix, 'fsdp', scatter_dimension=0, tiled=True)]
    all_gather x3 -> x2, waiting for transfers between devices: 201 us -> 0.04 us  [gather(): return lax.all_gather(shard, 'fsdp', axis=0, tiled=False)]
    ppermute x0 -> x47, waiting for transfers between devices: none -> 121 us  [hop(): return lax.ppermute(values, 'fsdp', pairs)]
    ppermute x0 -> x47, starting transfers between devices: none -> 60.5 us  [hop(): return lax.ppermute(values, 'fsdp', pairs)]
    reshape x8 -> x4, local copies, waits for them, and re-layouts: 32.1 us -> 2.35 us  [the longest x1 1.4 us: local(): small_all.reshape(4, 4, -1)]
    slice x24 -> x13, local copies, waits for them, and re-layouts: 27.2 us -> 3.94 us  [the longest x2 1.86 us: blocks_of(): matrix[:, at:at + D].reshape(owners, rows_of, D)]
    ppermute x7 -> x16, waiting for transfers between devices: 32 us -> 47.8 us  [swap_seq(): return lax.ppermute(values, 'seq', [(0, 1), (1, 0)])]
    convert_element_type x1 -> x16, other arithmetic: 0.01 us -> 15.1 us  [the longest x11 14.1 us: total(): return result.astype(BF16)]
  transfers between devices with their start and end apart: 13 -> 66, of which waited for: 9 -> 24; matrix products, arithmetic and copies ran while one was open for 20% -> 31% of each run, Pallas kernels for 2% -> 8%
where the time goes in v2:
time: 609 us; the launch traced here: 598 us
  waiting for transfers between devices  169 us (28%)
  matrix products  118 us (19%)
  local copies, waits for them, and re-layouts  91.9 us (15%)
  starting transfers between devices  78.3 us (13%)
  Pallas kernels  72.8 us (12%)
  other arithmetic  51.8 us (9%)
  between operations  16.8 us (3%)
    ppermute x47, waiting for transfers between devices, hop(): return lax.ppermute(values, 'fsdp', pairs)  121 us
    ppermute x47, starting transfers between devices, hop(): return lax.ppermute(values, 'fsdp', pairs)  60.5 us
    dot_general x22, matrix products, dot(): return jnp.dot(left_side, right_side, preferred_element_type=F32)  50.8 us
    ppermute x16, waiting for transfers between devices, swap_seq(): return lax.ppermute(values, 'seq', [(0, 1), (1, 0)])  47.8 us
    dot_general x12, matrix products, dot_back(): lax.dot_general(left_side, right_side, (((1,), (1,)), ((), ())), preferre...  38.7 us
    pallas_call x2, Pallas kernels, attend_back(): pl.pallas_call(attend_back_kernel, grid=(PAIRS,), in_specs=[whole((1, row...  38.2 us
    unnamed x326, local copies, waits for them, and re-layouts  30.6 us
    dot_general x10, matrix products, dot_rows(): lax.dot_general(left_side, right_side, (((0,), (0,)), ((), ())), preferre...  28.9 us
  transfers between devices with their start and end apart: 66, of which 24 were waited for; matrix products, arithmetic and copies ran while one was open for 31% of the time, Pallas kernels for 8%

profile of v2, /device:TPU:0, one launch (start us, length us, event | category | flops | bytes accessed | tf_op | source)
XLA Modules:
  0.0 598.5 jit_solution(5499877444248393961)
XLA Ops:
  17.2 5.1 collective-permute-start.2
  23.7 4.6 collective-permute-start.17
  58.4 18.4 %collective-permute-done.20 = bf16[48,3072]{1,0:T(8,128)(2,1)S(1)} collective-permute-done((bf16[48,3072]{1,0:T(8,128)(2,1)}, bf16[48,3072]{1,0:T(8,128)(2,1)S(1)}, u32[]{:S(2)}, u32[]{:S(2)}) %collective-permute-start.20) | collective-permute-done | bytes 294944 | tf_op jit(solution)/shard_map/gather1/down2/ppermute | solution.py:231
  79.2 10.4 %collective-permute-done.6 = bf16[48,3072]{1,0:T(8,128)(2,1)S(1)} collective-permute-done((bf16[48,3072]{1,0:T(8,128)(2,1)}, bf16[48,3072]{1,0:T(8,128)(2,1)S(1)}, u32[]{:S(2)}, u32[]{:S(2)}) %collective-permute-start.6) | collective-permute-done | bytes 294944 | tf_op jit(solution)/shard_map/gather0/down3/ppermute | solution.py:231
  99.1 11.7 %collective-permute-done.7 = bf16[4,48,1536]{2,1,0:T(8,128)(2,1)S(1)} collective-permute-done((bf16[4,48,1536]{2,1,0:T(8,128)(2,1)S(1)}, bf16[4,48,1536]{2,1,0:T(8,128)(2,1)S(1)}, u32[]{:S(2)}, u32[]{:S(2)}) %collective-permute-start.7) | collective-permute-done | bytes 589856 | tf_op jit(solution)/shard_map/gather0/y1/ppermute | solution.py:231
  129.0 12.0 %collective-permute-done.8.refs_1_ = bf16[8,48,1536]{2,1,0:T(8,128)(2,1)} collective-permute-done((bf16[8,48,1536]{2,1,0:T(8,128)(2,1)S(1)}, bf16[8,48,1536]{2,1,0:T(8,128)(2,1)}, u32[]{:S(2)}, u32[]{:S(2)}) %collective-permute-start.8) | collective-permute-done | bytes 1179680 | tf_op jit(solution)/shard_map/gather0/x2/ppermute | solution.py:205
  142.6 17.8 %collective-permute-done.12.refs_5_ = bf16[8,48,1536]{2,1,0:T(8,128)(2,1)} collective-permute-done((bf16[8,48,1536]{2,1,0:T(8,128)(2,1)}, bf16[8,48,1536]{2,1,0:T(8,128)(2,1)}, u32[]{:S(2)}, u32[]{:S(2)}) %collective-permute-start.12) | collective-permute-done | bytes 1179680 | tf_op jit(solution)/shard_map/gather0/y2/ppermute | solution.py:231
  169.0 4.2 fusion.12.kv_ref
  176.5 13.3 %attend.2 = (bf16[512,768]{1,0:T(8,128)(2,1)}, f32[6,2,512]{2,1,0:T(2,128)}) custom-call(s32[512,1]{1,0:T(8,128)} %copy.134.seg_col, s32[1,768]{1,0:T(1,128)} %broadcast_select_fusion.15.seg_row, s32[1,768]{1,0:T(1,128)} %broadcast_select_fusion.14.valid_row, bf16[512,768]{1,0:T(8,128)(2,1)} %add_convert_fusion.6.q_ref, bf16[512,1536]{1,0:T(8,128)(2,1)} %fusion.12.kv_ref, ...), custom_call_target="tpu_custom_call" | custom-call | flops 1006632960 | bytes 6291456 | tf_op jit(solution)/shard_map/attend/pallas_call | solution.py:94
  192.1 4.1 assemble.2
  200.0 5.8 multiply_convert_fusion.1
  213.5 4.3 fusion.13.kv_ref
  217.8 3.6 collective-permute-done.15
  224.2 13.5 %attend.3 = (bf16[512,768]{1,0:T(8,128)(2,1)}, f32[6,2,512]{2,1,0:T(2,128)}) custom-call(s32[512,1]{1,0:T(8,128)} %copy.134.seg_col, s32[1,768]{1,0:T(1,128)} %broadcast_select_fusion.15.seg_row, s32[1,768]{1,0:T(1,128)} %broadcast_select_fusion.14.valid_row, bf16[512,768]{1,0:T(8,128)(2,1)} %add_convert_fusion.3.q_ref, bf16[512,1536]{1,0:T(8,128)(2,1)} %fusion.13.kv_ref, ...), custom_call_target="tpu_custom_call" | custom-call | flops 1006632960 | bytes 6291456 | tf_op jit(solution)/shard_map/attend/pallas_call | solution.py:94
  242.3 3.8 assemble.3
  246.1 4.9 multiply_convert_fusion
  251.0 4.4 fusion.5
  272.9 19.2 %attend_back.2 = (bf16[512,768]{1,0:T(8,128)(2,1)}, bf16[512,1536]{1,0:T(8,128)(2,1)}, bf16[256,1536]{1,0:T(8,128)(2,1)}) custom-call(s32[1,512]{1,0:T(1,128)} %bitcast.463, s32[768,1]{1,0:T(8,128)} %get-tuple-element.191.seg_col, s32[768,1]{1,0:T(8,128)} %get-tuple-element.190.valid_col, bf16[512,768]{1,0:T(8,128)(2,1)} %add_convert_fusion.3.q_ref, ...), custom_call_target="tpu_custom_call" | custom-call | flops 2516582400 | bytes 10485760 | tf_op jit(solution)/shard_map/back1/attend_back/pallas_call | solution.py:178
  341.2 7.6 %fusion.11 = bf16[512,3072]{1,0:T(8,128)(2,1)S(1)} fusion(f32[512,3072]{1,0:T(8,128)} %get-tuple-element.181, bf16[3072,768]{1,0:T(8,128)(2,1)S(1)} %bitcast.400, f32[3072]{0:T(1024)S(1)} %copy-done.112, f32[512,768]{1,0:T(8,128)S(1)} %add_add_fusion.6), kind=kOutput, calls=%fused_computation.13 | convolution fusion | flops 2433613824 | bytes 15740928 | tf_op jit(solution)/shard_map/dot_general | solution.py:47
  348.8 4.0 multiply_reduce_fusion.2
  365.2 6.5 %convolution_convert_fusion.2._ = bf16[768,3072]{1,0:T(8,128)(2,1)} fusion(bf16[512,3072]{1,0:T(8,128)(2,1)} %copy-done.38, f32[512,768]{1,0:T(8,128)S(1)} %copy-done.26, f32[768]{0:T(1024)S(1)} %copy-done.121, f32[768]{0:T(1024)S(1)} %copy-done.109, f32[512]{0:T(512)S(1)} %copy-done.117, f32[512]{0:T(512)S(1)} %copy-done.95), kind=kOutput, calls=%fused_computation.20 | convolution fusion | flops 2420244480 | bytes 9447424 | tf_op jit(solution)/shard_map/dot_general | solution.py:43
  371.7 19.0 %attend_back.3 = (bf16[512,768]{1,0:T(8,128)(2,1)}, bf16[512,1536]{1,0:T(8,128)(2,1)}, bf16[256,1536]{1,0:T(8,128)(2,1)}) custom-call(s32[1,512]{1,0:T(1,128)} %bitcast.464, s32[768,1]{1,0:T(8,128)} %get-tuple-element.191.seg_col, s32[768,1]{1,0:T(8,128)} %get-tuple-element.190.valid_col, bf16[512,768]{1,0:T(8,128)(2,1)} %add_convert_fusion.6.q_ref, ...), custom_call_target="tpu_custom_call" | custom-call | flops 2516582400 | bytes 10485760 | tf_op jit(solution)/shard_map/back0/attend_back/pallas_call | solution.py:178
  406.0 4.2 convolution_convert_fusion.5
  439.9 19.5 %collective-permute-done.40 = f32[16,1152]{1,0:T(8,128)S(1)} collective-permute-done((f32[16,1152]{1,0:T(8,128)S(1)}, f32[16,1152]{1,0:T(8,128)S(1)}, u32[]{:S(2)}, u32[]{:S(2)}) %collective-permute-start.40) | collective-permute-done | bytes 73760 | tf_op jit(solution)/shard_map/small/ppermute | solution.py:231
  488.2 4.4 collective-permute-start.44
  493.3 14.8 %collective-permute-done.54 = bf16[4,192,768]{2,1,0:T(8,128)(2,1)S(1)} collective-permute-done((bf16[4,192,768]{2,1,0:T(8,128)(2,1)S(1)}, bf16[4,192,768]{2,1,0:T(8,128)(2,1)S(1)}, u32[]{:S(2)}, u32[]{:S(2)}) %collective-permute-start.54) | collective-permute-done | bytes 1179680 | tf_op jit(solution)/shard_map/feed/y1/ppermute | solution.py:231
  514.3 8.1 %collective-permute-done.55 = bf16[4,192,384]{2,1,0:T(8,128)(2,1)S(1)} collective-permute-done((bf16[4,192,384]{2,1,0:T(8,128)(2,1)S(1)}, bf16[4,192,384]{2,1,0:T(8,128)(2,1)S(1)}, u32[]{:S(2)}, u32[]{:S(2)}) %collective-permute-start.55) | collective-permute-done | bytes 589856 | tf_op jit(solution)/shard_map/feed/x2/ppermute | solution.py:205
  530.9 4.4 collective-permute-start.57
  541.4 4.1 collective-permute-start.58
  549.7 9.8 %collective-permute-done.61 = bf16[48,3072]{1,0:T(8,128)(2,1)S(1)} collective-permute-done((bf16[48,3072]{1,0:T(8,128)(2,1)S(1)}, bf16[48,3072]{1,0:T(8,128)(2,1)S(1)}, u32[]{:S(2)}, u32[]{:S(2)}) %collective-permute-start.61) | collective-permute-done | bytes 294944 | tf_op jit(solution)/shard_map/feed/down1/ppermute | solution.py:231
  561.1 8.5 %collective-permute-done.62 = bf16[48,3072]{1,0:T(8,128)(2,1)S(1)} collective-permute-done((bf16[48,3072]{1,0:T(8,128)(2,1)S(1)}, bf16[48,3072]{1,0:T(8,128)(2,1)S(1)}, u32[]{:S(2)}, u32[]{:S(2)}) %collective-permute-start.62) | collective-permute-done | bytes 294944 | tf_op jit(solution)/shard_map/feed_last/ppermute | solution.py:205
  571.2 11.7 %collective-permute-done.49 = bf16[576,768]{1,0:T(8,128)(2,1)S(1)} collective-permute-done((bf16[576,768]{1,0:T(8,128)(2,1)}, bf16[576,768]{1,0:T(8,128)(2,1)S(1)}, u32[]{:S(2)}, u32[]{:S(2)}) %collective-permute-start.49) | collective-permute-done | bytes 884768 | tf_op jit(solution)/shard_map/ppermute | solution.py:205
  (712 shorter events, 294.2 us)
Async XLA Ops:
  7.2 110.2 %all-gather.5.cloned.1.call-start = ((), (), s32[]{:S(2)}) async-start(), calls=%async_computation.2 | async-start | bytes 5222400 | tf_op jit(solution)/shard_map/mixing0/all_gather | solution.py:454
  16.7 193.5 %all-gather.7.cloned.1.call-start = ((), (), s32[]{:S(2)}) async-start(), calls=%async_computation.3 | async-start | bytes 5013504 | tf_op jit(solution)/shard_map/mixing1/all_gather | solution.py:454
  30.8 538.9 %reduce-scatter.2.cloned.1.call-start = ((), (), s32[]{:S(2)}) async-start(), calls=%async_computation.1 | async-start | bytes 15040512 | tf_op jit(solution)/shard_map/scatter1/reduce_scatter | solution.py:516
  50.4 26.4 %collective-permute-start.20 = (bf16[48,3072]{1,0:T(8,128)(2,1)}, bf16[48,3072]{1,0:T(8,128)(2,1)S(1)}, u32[]{:S(2)}, u32[]{:S(2)}) collective-permute-start(bf16[48,3072]{1,0:T(8,128)(2,1)} %collective-permute-done.16), channel_id=1, source_target_pairs={{4,0},{5,1},{6,2},{7,3},{8,4},{9,5},{10,6},{11,7},{20,16},{21,17},... | collective-permute-start | bytes 884744 | tf_op jit(solution)/shard_map/gather1/down2/ppermute | solution.py:231
  51.7 26.5 %collective-permute-start.4 = (bf16[48,3072]{1,0:T(8,128)(2,1)}, bf16[48,3072]{1,0:T(8,128)(2,1)S(1)}, u32[]{:S(2)}, u32[]{:S(2)}) collective-permute-start(bf16[48,3072]{1,0:T(8,128)(2,1)} %collective-permute-done.3), channel_id=1, source_target_pairs={{8,12},{9,13},{10,14},{11,15},{24,28},{25,29},{26,30},{27,31}} | collective-permute-start | bytes 884744 | tf_op jit(solution)/shard_map/gather0/up3/ppermute | solution.py:231
  56.4 33.2 %collective-permute-start.6 = (bf16[48,3072]{1,0:T(8,128)(2,1)}, bf16[48,3072]{1,0:T(8,128)(2,1)S(1)}, u32[]{:S(2)}, u32[]{:S(2)}) collective-permute-start(bf16[48,3072]{1,0:T(8,128)(2,1)} %collective-permute-done.5), channel_id=1, source_target_pairs={{4,0},{5,1},{6,2},{7,3},{20,16},{21,17},{22,18},{23,19}} | collective-permute-start | bytes 884744 | tf_op jit(solution)/shard_map/gather0/down3/ppermute | solution.py:231
  57.7 35.2 %collective-permute-start.19 = (bf16[48,3072]{1,0:T(8,128)(2,1)S(1)}, bf16[48,3072]{1,0:T(8,128)(2,1)S(1)}, u32[]{:S(2)}, u32[]{:S(2)}) collective-permute-start(bf16[48,3072]{1,0:T(8,128)(2,1)S(1)} %collective-permute-done.18), channel_id=1, source_target_pairs={{8,12},{9,13},{10,14},{11,15},{24,28},{25,29},{26,30},{27,31}} | collective-permute-start | bytes 884744 | tf_op jit(solution)/shard_map/gather1/up3/ppermute | solution.py:231
  97.6 25.8 %collective-permute-start.22 = (bf16[4,48,1536]{2,1,0:T(8,128)(2,1)}, bf16[4,48,1536]{2,1,0:T(8,128)(2,1)}, u32[]{:S(2)}, u32[]{:S(2)}) collective-permute-start(bf16[4,48,1536]{2,1,0:T(8,128)(2,1)} %get-tuple-element.112), channel_id=1, source_target_pairs={{0,2},{1,3},{2,0},{3,1},{4,6},{5,7},{6,4},{7,5},{8,10},{9,11},{10,... | collective-permute-start | bytes 1769480 | tf_op jit(solution)/shard_map/gather1/y1/ppermute | solution.py:231
  111.0 30.0 %collective-permute-start.8 = (bf16[8,48,1536]{2,1,0:T(8,128)(2,1)S(1)}, bf16[8,48,1536]{2,1,0:T(8,128)(2,1)}, u32[]{:S(2)}, u32[]{:S(2)}) collective-permute-start(bf16[8,48,1536]{2,1,0:T(8,128)(2,1)S(1)} %pad_maximum_fusion.3.refs_0_), channel_id=1, source_target_pairs={{0,16},{16,0},{1,17},{17,1},{2,18},{18,2},{3,19},{19,3},{4,20},{20... | collective-permute-start | bytes 3538952 | tf_op jit(solution)/shard_map/gather0/x2/ppermute | solution.py:205
  112.7 77.2 %collective-permute-start.13 = (bf16[8,48,1536]{2,1,0:T(8,128)(2,1)}, bf16[8,48,1536]{2,1,0:T(8,128)(2,1)}, u32[]{:S(2)}, u32[]{:S(2)}) collective-permute-start(bf16[8,48,1536]{2,1,0:T(8,128)(2,1)} %pad_maximum_fusion.4.refs_4_), channel_id=1, source_target_pairs={{0,1},{1,0},{2,3},{3,2},{4,5},{5,4},{6,7},{7,6},{8,9},{9,8},{10,11... | collective-permute-start | bytes 3538952 | tf_op jit(solution)/shard_map/gather0/c2/ppermute | solution.py:231
  115.6 44.8 %collective-permute-start.12 = (bf16[8,48,1536]{2,1,0:T(8,128)(2,1)}, bf16[8,48,1536]{2,1,0:T(8,128)(2,1)}, u32[]{:S(2)}, u32[]{:S(2)}) collective-permute-start(bf16[8,48,1536]{2,1,0:T(8,128)(2,1)} %pad_maximum_fusion.4.refs_4_), channel_id=1, source_target_pairs={{0,2},{1,3},{2,0},{3,1},{4,6},{5,7},{6,4},{7,5},{8,10},{9,11},{10,... | collective-permute-start | bytes 3538952 | tf_op jit(solution)/shard_map/gather0/y2/ppermute | solution.py:231
  124.2 36.3 %collective-permute-start = (bf16[256,768]{1,0:T(8,128)(2,1)S(1)}, bf16[256,768]{1,0:T(8,128)(2,1)S(1)}, u32[]{:S(2)}, u32[]{:S(2)}) collective-permute-start(bf16[256,768]{1,0:T(8,128)(2,1)S(1)} %slice.640), channel_id=1, source_target_pairs={{0,16},{16,0},{1,17},{17,1},{2,18},{18,2},{3,19},{19,3},{4,20},{20... | collective-permute-start | bytes 1179656 | tf_op jit(solution)/shard_map/ppermute | solution.py:205
  128.9 61.2 %collective-permute-start.23 = (bf16[8,48,1536]{2,1,0:T(8,128)(2,1)S(1)}, bf16[8,48,1536]{2,1,0:T(8,128)(2,1)}, u32[]{:S(2)}, u32[]{:S(2)}) collective-permute-start(bf16[8,48,1536]{2,1,0:T(8,128)(2,1)S(1)} %pad_maximum_fusion.6.refs_0_), channel_id=1, source_target_pairs={{0,16},{16,0},{1,17},{17,1},{2,18},{18,2},{3,19},{19,3},{4,20},{20... | collective-permute-start | bytes 3538952 | tf_op jit(solution)/shard_map/gather1/x2/ppermute | solution.py:205
  141.0 49.5 %collective-permute-start.27 = (bf16[8,48,1536]{2,1,0:T(8,128)(2,1)S(1)}, bf16[8,48,1536]{2,1,0:T(8,128)(2,1)}, u32[]{:S(2)}, u32[]{:S(2)}) collective-permute-start(bf16[8,48,1536]{2,1,0:T(8,128)(2,1)S(1)} %pad_maximum_fusion.7.refs_4_), channel_id=1, source_target_pairs={{0,2},{1,3},{2,0},{3,1},{4,6},{5,7},{6,4},{7,5},{8,10},{9,11},{10,... | collective-permute-start | bytes 3538952 | tf_op jit(solution)/shard_map/gather1/y2/ppermute | solution.py:231
  160.4 30.2 %collective-permute-start.10 = (bf16[8,48,1536]{2,1,0:T(8,128)(2,1)}, bf16[8,48,1536]{2,1,0:T(8,128)(2,1)}, u32[]{:S(2)}, u32[]{:S(2)}) collective-permute-start(bf16[8,48,1536]{2,1,0:T(8,128)(2,1)} %collective-permute-done.8.refs_1_), channel_id=1, source_target_pairs={{0,1},{1,0},{2,3},{3,2},{4,5},{5,4},{6,7},{7,6},{8,9},{9,8},{10,11... | collective-permute-start | bytes 3538952 | tf_op jit(solution)/shard_map/gather0/c3/ppermute | solution.py:231
  160.5 30.5 %collective-permute-start.14 = (bf16[8,48,1536]{2,1,0:T(8,128)(2,1)}, bf16[8,48,1536]{2,1,0:T(8,128)(2,1)}, u32[]{:S(2)}, u32[]{:S(2)}) collective-permute-start(bf16[8,48,1536]{2,1,0:T(8,128)(2,1)} %collective-permute-done.12.refs_5_), channel_id=1, source_target_pairs={{0,1},{1,0},{2,3},{3,2},{4,5},{5,4},{6,7},{7,6},{8,9},{9,8},{10,11... | collective-permute-start | bytes 3538952 | tf_op jit(solution)/shard_map/gather0/c4/ppermute | solution.py:231
  189.9 51.0 %collective-permute-start.24 = (bf16[8,48,1536]{2,1,0:T(8,128)(2,1)S(1)}, bf16[8,48,1536]{2,1,0:T(8,128)(2,1)}, u32[]{:S(2)}, u32[]{:S(2)}) collective-permute-start(bf16[8,48,1536]{2,1,0:T(8,128)(2,1)S(1)} %pad_maximum_fusion.6.refs_0_), channel_id=1, source_target_pairs={{0,1},{1,0},{2,3},{3,2},{4,5},{5,4},{6,7},{7,6},{8,9},{9,8},{10,11... | collective-permute-start | bytes 3538952 | tf_op jit(solution)/shard_map/gather1/c1/ppermute | solution.py:231
  190.1 50.9 %collective-permute-start.28 = (bf16[8,48,1536]{2,1,0:T(8,128)(2,1)S(1)}, bf16[8,48,1536]{2,1,0:T(8,128)(2,1)}, u32[]{:S(2)}, u32[]{:S(2)}) collective-permute-start(bf16[8,48,1536]{2,1,0:T(8,128)(2,1)S(1)} %pad_maximum_fusion.7.refs_4_), channel_id=1, source_target_pairs={{0,1},{1,0},{2,3},{3,2},{4,5},{5,4},{6,7},{7,6},{8,9},{9,8},{10,11... | collective-permute-start | bytes 3538952 | tf_op jit(solution)/shard_map/gather1/c2/ppermute | solution.py:231
  190.5 50.5 %collective-permute-start.25 = (bf16[8,48,1536]{2,1,0:T(8,128)(2,1)}, bf16[8,48,1536]{2,1,0:T(8,128)(2,1)}, u32[]{:S(2)}, u32[]{:S(2)}) collective-permute-start(bf16[8,48,1536]{2,1,0:T(8,128)(2,1)} %collective-permute-done.23.refs_1_), channel_id=1, source_target_pairs={{0,1},{1,0},{2,3},{3,2},{4,5},{5,4},{6,7},{7,6},{8,9},{9,8},{10,11... | collective-permute-start | bytes 3538952 | tf_op jit(solution)/shard_map/gather1/c3/ppermute | solution.py:231
  190.6 50.4 %collective-permute-start.29 = (bf16[8,48,1536]{2,1,0:T(8,128)(2,1)}, bf16[8,48,1536]{2,1,0:T(8,128)(2,1)}, u32[]{:S(2)}, u32[]{:S(2)}) collective-permute-start(bf16[8,48,1536]{2,1,0:T(8,128)(2,1)} %collective-permute-done.27.refs_5_), channel_id=1, source_target_pairs={{0,1},{1,0},{2,3},{3,2},{4,5},{5,4},{6,7},{7,6},{8,9},{9,8},{10,11... | collective-permute-start | bytes 3538952 | tf_op jit(solution)/shard_map/gather1/c4/ppermute | solution.py:231
  303.8 30.6 %collective-permute-start.30 = (bf16[256,768]{1,0:T(8,128)(2,1)}, bf16[256,768]{1,0:T(8,128)(2,1)}, u32[]{:S(2)}, u32[]{:S(2)}) collective-permute-start(bf16[256,768]{1,0:T(8,128)(2,1)} %fusion.45), channel_id=1, source_target_pairs={{0,16},{16,0},{1,17},{17,1},{2,18},{18,2},{3,19},{19,3},{4,20},{20... | collective-permute-start | bytes 1179656 | tf_op jit(solution)/shard_map/ppermute | solution.py:205
  396.2 27.8 %collective-permute-start.31 = (bf16[256,768]{1,0:T(8,128)(2,1)}, bf16[256,768]{1,0:T(8,128)(2,1)S(1)}, u32[]{:S(2)}, u32[]{:S(2)}) collective-permute-start(bf16[256,768]{1,0:T(8,128)(2,1)} %fusion.42), channel_id=1, source_target_pairs={{0,16},{16,0},{1,17},{17,1},{2,18},{18,2},{3,19},{19,3},{4,20},{20... | collective-permute-start | bytes 1179656 | tf_op jit(solution)/shard_map/ppermute | solution.py:205
  399.3 31.7 %collective-permute-start.36 = (bf16[8,48,768]{2,1,0:T(8,128)(2,1)}, bf16[8,48,768]{2,1,0:T(8,128)(2,1)}, u32[]{:S(2)}, u32[]{:S(2)}) collective-permute-start(bf16[8,48,768]{2,1,0:T(8,128)(2,1)} %get-tuple-element.109), channel_id=1, source_target_pairs={{0,1},{1,0},{2,3},{3,2},{4,5},{5,4},{6,7},{7,6},{8,9},{9,8},{10,11... | collective-permute-start | bytes 1769480 | tf_op jit(solution)/shard_map/mix_core/ppermute | solution.py:231
  401.9 29.6 %collective-permute-start.35 = (bf16[8,48,768]{2,1,0:T(8,128)(2,1)}, bf16[8,48,768]{2,1,0:T(8,128)(2,1)}, u32[]{:S(2)}, u32[]{:S(2)}) collective-permute-start(bf16[8,48,768]{2,1,0:T(8,128)(2,1)} %get-tuple-element.107), channel_id=1, source_target_pairs={{0,1},{1,0},{2,3},{3,2},{4,5},{5,4},{6,7},{7,6},{8,9},{9,8},{10,11... | collective-permute-start | bytes 1769480 | tf_op jit(solution)/shard_map/mix_core/ppermute | solution.py:231
  411.3 23.4 %collective-permute-start.32 = (bf16[8,48,1536]{2,1,0:T(8,128)(2,1)}, bf16[8,48,1536]{2,1,0:T(8,128)(2,1)}, u32[]{:S(2)}, u32[]{:S(2)}) collective-permute-start(bf16[8,48,1536]{2,1,0:T(8,128)(2,1)} %dynamic-slice_bitcast_fusion.2), channel_id=1, source_target_pairs={{0,1},{1,0},{2,3},{3,2},{4,5},{5,4},{6,7},{7,6},{8,9},{9,8},{10,11... | collective-permute-start | bytes 3538952 | tf_op jit(solution)/shard_map/mix_core/ppermute | solution.py:231
  412.9 64.4 %collective-permute-start.50 = (bf16[8,48,3072]{2,1,0:T(8,128)(2,1)}, bf16[8,48,3072]{2,1,0:T(8,128)(2,1)}, u32[]{:S(2)}, u32[]{:S(2)}) collective-permute-start(bf16[8,48,3072]{2,1,0:T(8,128)(2,1)} %dynamic-slice_bitcast_fusion.1), channel_id=1, source_target_pairs={{0,1},{1,0},{2,3},{3,2},{4,5},{5,4},{6,7},{7,6},{8,9},{9,8},{10,11... | collective-permute-start | bytes 7077896 | tf_op jit(solution)/shard_map/feed_core/ppermute | solution.py:231
  424.1 56.2 %collective-permute-start.53 = (bf16[8,192,768]{2,1,0:T(8,128)(2,1)}, bf16[8,192,768]{2,1,0:T(8,128)(2,1)}, u32[]{:S(2)}, u32[]{:S(2)}) collective-permute-start(bf16[8,192,768]{2,1,0:T(8,128)(2,1)} %get-tuple-element.82), channel_id=1, source_target_pairs={{0,1},{1,0},{2,3},{3,2},{4,5},{5,4},{6,7},{7,6},{8,9},{9,8},{10,11... | collective-permute-start | bytes 7077896 | tf_op jit(solution)/shard_map/feed_core/ppermute | solution.py:231
  433.0 28.5 %collective-permute-start.37 = (bf16[4,48,1536]{2,1,0:T(8,128)(2,1)S(1)}, bf16[4,48,1536]{2,1,0:T(8,128)(2,1)S(1)}, u32[]{:S(2)}, u32[]{:S(2)}) collective-permute-start(bf16[4,48,1536]{2,1,0:T(8,128)(2,1)S(1)} %fusion.71), channel_id=1, source_target_pairs={{0,2},{1,3},{2,0},{3,1},{4,6},{5,7},{6,4},{7,5},{8,10},{9,11},{10,... | collective-permute-start | bytes 1769480 | tf_op jit(solution)/shard_map/mix/y1/ppermute | solution.py:231
  436.3 27.5 %collective-permute-start.33 = (bf16[8,48,768]{2,1,0:T(8,128)(2,1)S(1)}, bf16[8,48,768]{2,1,0:T(8,128)(2,1)S(1)}, u32[]{:S(2)}, u32[]{:S(2)}) collective-permute-start(bf16[8,48,768]{2,1,0:T(8,128)(2,1)S(1)} %fusion.55), channel_id=1, source_target_pairs={{0,16},{16,0},{1,17},{17,1},{2,18},{18,2},{3,19},{19,3},{4,20},{20... | collective-permute-start | bytes 1769480 | tf_op jit(solution)/shard_map/mix/x1/ppermute | solution.py:205
  479.6 31.7 %collective-permute-start.51 = (bf16[8,48,1536]{2,1,0:T(8,128)(2,1)S(1)}, bf16[8,48,1536]{2,1,0:T(8,128)(2,1)S(1)}, u32[]{:S(2)}, u32[]{:S(2)}) collective-permute-start(bf16[8,48,1536]{2,1,0:T(8,128)(2,1)S(1)} %fusion.20), channel_id=1, source_target_pairs={{0,16},{16,0},{1,17},{17,1},{2,18},{18,2},{3,19},{19,3},{4,20},{20... | collective-permute-start | bytes 3538952 | tf_op jit(solution)/shard_map/feed/x1/ppermute | solution.py:205
  481.9 26.1 %collective-permute-start.54 = (bf16[4,192,768]{2,1,0:T(8,128)(2,1)S(1)}, bf16[4,192,768]{2,1,0:T(8,128)(2,1)S(1)}, u32[]{:S(2)}, u32[]{:S(2)}) collective-permute-start(bf16[4,192,768]{2,1,0:T(8,128)(2,1)S(1)} %fusion.48), channel_id=1, source_target_pairs={{0,2},{1,3},{2,0},{3,1},{4,6},{5,7},{6,4},{7,5},{8,10},{9,11},{10,... | collective-permute-start | bytes 3538952 | tf_op jit(solution)/shard_map/feed/y1/ppermute | solution.py:231
  488.2 38.5 %collective-permute-start.44 = (bf16[48,1664]{1,0:T(8,128)(2,1)S(1)}, bf16[48,1664]{1,0:T(8,128)(2,1)S(1)}, u32[]{:S(2)}, u32[]{:S(2)}) collective-permute-start(bf16[48,1664]{1,0:T(8,128)(2,1)S(1)} %get-tuple-element.121), channel_id=1, source_target_pairs={{0,4},{1,5},{2,6},{3,7},{4,8},{5,9},{6,10},{7,11},{8,12},{9,13},{1... | collective-permute-start | bytes 479240 | tf_op jit(solution)/shard_map/mix/up1/ppermute | solution.py:231
  (188 other events, 1407.1 us)
Sparse Core Ops, SparseCore 0:
  16.8 71.0 all-gather.4
  90.8 68.8 all-gather.6
  322.9 148.4 reduce-scatter.1
